TPU v7x, 32 devices: a whole 2x2x4 slice. The times are simulated.
32 devices in a mesh: rep: 8 (over y, x, core), shard: 4 (over z).
Axes of the slice: x: 2, y: 2, z: 4, core: 2. Of those that a mesh axis runs over, the one named last changes fastest.
Arguments:
- tokens: bfloat16 [32, 512, 1024], P(('rep', 'shard')), may hold values from -6 to 6
- segments: int32 [32, 512], P(('rep', 'shard')), may hold values from 0 to 25, as said below
- lengths: int32 [32], P(('rep', 'shard')), may hold values from 449 to 512, as said below
- cotangent: bfloat16 [32, 512, 1024], P(('rep', 'shard')), may hold values from -6 to 6
- w_qkv: bfloat16 [1024, 3072], P('shard'), may hold values from -0.1875 to 0.1875
- b_qv: bfloat16 [2048], P('shard'), may hold values from -4 to 4
- w_out: bfloat16 [1024, 1024], P('shard'), may hold values from -0.5 to 0.5
- b_out: bfloat16 [1024], P('shard'), may hold values from -4 to 4
- gain_one: bfloat16 [1024], P('shard'), may hold values from 0.5 to 1.5
- shift_one: bfloat16 [1024], P('shard'), may hold values from -4 to 4
- w_in: bfloat16 [1024, 4096], P('shard'), may hold values from -0.1875 to 0.1875
- b_in: bfloat16 [4096], P('shard'), may hold values from -4 to 4
- w_down: bfloat16 [4096, 1024], P('shard'), may hold values from -0.09375 to 0.09375
- b_down: bfloat16 [1024], P('shard'), may hold values from -4 to 4
- gain_two: bfloat16 [1024], P('shard'), may hold values from 0.5 to 1.5
- shift_two: bfloat16 [1024], P('shard'), may hold values from -4 to 4
Outputs:
- layer_out: bfloat16 [32, 512, 1024], P(('rep', 'shard'))
- grad_tokens: float32 [32, 512, 1024], P(('rep', 'shard'))
- grad_w_qkv: float32 [1024, 3072], P('shard')
- grad_b_qv: float32 [2048], P('shard')
- grad_w_out: float32 [1024, 1024], P('shard')
- grad_b_out: float32 [1024], P('shard')
- grad_gain_one: float32 [1024], P('shard')
- grad_shift_one: float32 [1024], P('shard')
- grad_w_in: float32 [1024, 4096], P('shard')
- grad_b_in: float32 [4096], P('shard')
- grad_w_down: float32 [4096, 1024], P('shard')
- grad_b_down: float32 [1024], P('shard')
- grad_gain_two: float32 [1024], P('shard')
- grad_shift_two: float32 [1024], P('shard')
Inputs may be any that keep to these rules, and one draw needn't show every extreme that they name: `segments`: within a sequence the document numbers start at 0 and never fall; every document spans 20 to 200 positions unless the sequence's end cuts it; the first sequence is made of documents of 20 positions. `lengths`: positions from a sequence's length on are padding; the first sequence has none, the second has the most.
All inputs are finite; a program needn't handle non-finite values.
Results may differ from a plain program's by a relative error of at most 0.019.
Values may be sent and summed in bfloat16 or wider, within the bound.
No kernel may reach another device: no remote copies, remote signals or barrier semaphores. Data moves between devices by JAX's collectives and lax.ppermute only.
A program may use at most 192 MiB of HBM per device.

v0:
```python
from functools import partial
import jax
import jax.numpy as jnp
from jax import lax
from jax.sharding import Mesh
from jax.sharding import PartitionSpec as P

HEAD_DIM = 64
REP = ("chip", "core")
ALL = ("chip", "core", "shard")


def layer_norm(hidden, norm_gain, norm_shift):
    average = jnp.mean(hidden, axis=-1, keepdims=True)
    centred = hidden - average
    variance = jnp.mean(centred * centred, axis=-1, keepdims=True)
    return centred * lax.rsqrt(variance + 1e-06) * norm_gain + norm_shift


def matmul(left, right):
    return jnp.dot(left, right, preferred_element_type=jnp.float32)


def project_back(left, right):
    return lax.dot_general(
        left, right, (((1,), (1,)), ((), ())), preferred_element_type=jnp.float32
    )


def outer_sum(left, right):
    return lax.dot_general(
        left, right, (((0,), (0,)), ((), ())), preferred_element_type=jnp.float32
    )


def column_sum(values):
    return jnp.sum(values.astype(jnp.float32), axis=0)


def allowed_pairs(doc_ids, length):
    positions = jnp.arange(doc_ids.shape[0])
    is_valid = positions < length
    return (doc_ids[:, None] == doc_ids[None, :]) & (is_valid[:, None] == is_valid[None, :])


def attend(query_heads, key_heads, value_heads, allowed):
    scale = HEAD_DIM ** (-0.5)
    scores = (
        jnp.einsum("qhd,khd->hqk", query_heads, key_heads, preferred_element_type=jnp.float32)
        * scale
    )
    scores = jnp.where(allowed[None], scores, -1e30)
    maxima = jnp.max(scores, axis=2, keepdims=True)
    expo = jnp.exp(scores - maxima)
    totals = jnp.sum(expo, axis=2, keepdims=True)
    attn_probs = (expo / totals).astype(jnp.bfloat16)
    context = jnp.einsum(
        "hqk,khd->qhd", attn_probs, value_heads, preferred_element_type=jnp.float32
    )
    return (context.astype(jnp.bfloat16), maxima + jnp.log(totals))


def attend_back(query_heads, key_heads, value_heads, grad_context, allowed, log_totals):
    scale = HEAD_DIM ** (-0.5)
    scores = (
        jnp.einsum("qhd,khd->hqk", query_heads, key_heads, preferred_element_type=jnp.float32)
        * scale
    )
    scores = jnp.where(allowed[None], scores, -1e30)
    attn_probs = jnp.exp(scores - log_totals)
    grad_probs = jnp.einsum(
        "qhd,khd->hqk", grad_context, value_heads, preferred_element_type=jnp.float32
    )
    grad_scores = attn_probs * (
        grad_probs - jnp.sum(attn_probs * grad_probs, axis=2, keepdims=True)
    )
    grad_low = grad_scores.astype(jnp.bfloat16)
    grad_query = (
        jnp.einsum("hqk,khd->qhd", grad_low, key_heads, preferred_element_type=jnp.float32) * scale
    )
    grad_key = (
        jnp.einsum("hqk,qhd->khd", grad_low, query_heads, preferred_element_type=jnp.float32)
        * scale
    )
    grad_value = jnp.einsum(
        "hqk,qhd->khd",
        attn_probs.astype(jnp.bfloat16),
        grad_context,
        preferred_element_type=jnp.float32,
    )
    return (
        grad_query.astype(jnp.bfloat16),
        grad_key.astype(jnp.bfloat16),
        grad_value.astype(jnp.bfloat16),
    )


def local(
    chips,
    group,
    tokens,
    segments,
    lengths,
    cotangent,
    w_qkv,
    b_qv,
    w_out,
    b_out,
    gain_one,
    shift_one,
    w_in,
    b_in,
    w_down,
    b_down,
    gain_two,
    shift_two,
):
    reps = 2 * chips
    core = lax.axis_index("core")
    rank = lax.axis_index("chip") * 2 + core
    own = lax.axis_index("shard")
    _, seq_len, model_width = tokens.shape
    num_heads = model_width // HEAD_DIM
    split_shape = (seq_len, num_heads, HEAD_DIM)
    ff_rows = w_down.shape[0]
    ff_width = w_in.shape[1]
    qkv_width = w_qkv.shape[1]

    def from_shard(value, step):
        return lax.ppermute(value, "shard", [(i, (i - step) % group) for i in range(group)])

    def to_shard(value, step):
        return lax.ppermute(value, "shard", [(i, (i + step) % group) for i in range(group)])

    def sibling(value):
        return lax.ppermute(value, "core", [(0, 1), (1, 0)])

    def roll_left(value, width):
        twice = jnp.concatenate([value, value], axis=1)
        return lax.dynamic_slice_in_dim(twice, own * width, value.shape[1], axis=1)

    def roll_right(value, width):
        twice = jnp.concatenate([value, value], axis=1)
        start = (group - own) % group * width
        return lax.dynamic_slice_in_dim(twice, start, value.shape[1], axis=1)

    vectors = (b_qv, b_out, gain_one, shift_one, b_in, b_down, gain_two, shift_two)
    sizes = [v.shape[0] for v in vectors]
    w_one = jnp.concatenate([w_qkv, w_out], axis=1)
    part = w_one.shape[1] // reps
    rows = w_one.shape[0]
    packed = jnp.concatenate(vectors)
    extra = -(-packed.shape[0] // (16 * part)) * 16
    packed = jnp.pad(packed, (0, extra * part - packed.shape[0])).reshape(extra, part)
    piece_one = jnp.concatenate(
        [lax.dynamic_slice_in_dim(w_one, rank * part, part, axis=1), packed], axis=0
    )
    part_in = ff_width // reps
    piece_in = lax.dynamic_slice_in_dim(w_in, rank * part_in, part_in, axis=1)
    part_down = ff_rows // reps
    piece_down = lax.dynamic_slice_in_dim(w_down, rank * part_down, part_down, axis=0)
    got_one = [from_shard(piece_one, s) for s in range(1, group)]
    got_in = [from_shard(piece_in, s) for s in range(1, group)]
    got_down = [from_shard(piece_down, s) for s in range(1, group)]
    rest_one = lax.all_gather(
        jnp.concatenate([g[:rows] for g in got_one], axis=0), REP, axis=1, tiled=True
    )
    rest_in = lax.all_gather(jnp.concatenate(got_in, axis=0), REP, axis=1, tiled=True)
    rest_down = lax.all_gather(jnp.stack(got_down), REP, axis=1, tiled=True)
    rest_down = rest_down.reshape(-1, model_width)
    relative = jnp.stack([packed.reshape(-1)] + [g[rows:].reshape(-1) for g in got_one])
    natural = jnp.concatenate([relative, relative], axis=0)
    natural = lax.dynamic_slice_in_dim(natural, (group - own) % group, group, axis=0)
    full, start = ([], 0)
    for size in sizes:
        full.append(natural[:, start : start + size].reshape(-1).astype(jnp.float32))
        start += size
    bias_qv, bias_out, norm_gone, norm_sone, bias_in, bias_down, norm_gtwo, norm_stwo = full
    own_qkv, own_out = (w_qkv, w_out)
    rest_qkv, rest_out = (rest_one[:, :qkv_width], rest_one[:, qkv_width:])
    flat_in = tokens[0]
    in_rel = roll_left(flat_in, rows)
    projected = matmul(in_rel[:, :rows], own_qkv) + matmul(in_rel[:, rows:], rest_qkv)
    queries = (projected[:, :model_width] + bias_qv[:model_width]).astype(jnp.bfloat16)
    key_rows = projected[:, model_width : 2 * model_width].astype(jnp.bfloat16)
    value_rows = (projected[:, 2 * model_width :] + bias_qv[model_width:]).astype(jnp.bfloat16)
    query_heads = queries.reshape(split_shape)
    key_heads = key_rows.reshape(split_shape)
    value_heads = value_rows.reshape(split_shape)
    allowed = allowed_pairs(segments[0], lengths[0])
    context, log_totals = attend(query_heads, key_heads, value_heads, allowed)
    context_rel = roll_left(context.reshape(-1, model_width), rows)
    attn_out = (
        matmul(context_rel[:, :rows], own_out) + matmul(context_rel[:, rows:], rest_out) + bias_out
    )
    first_sum = flat_in.astype(jnp.float32) + attn_out
    normed_one = layer_norm(first_sum, norm_gone, norm_sone)
    normed_rel = roll_left(normed_one.astype(jnp.bfloat16), rows)
    inner = matmul(normed_rel[:, :rows], w_in) + matmul(normed_rel[:, rows:], rest_in) + bias_in
    activated = jax.nn.gelu(inner, approximate=False)
    act_rel = roll_left(activated.astype(jnp.bfloat16), ff_rows)
    branch = (
        matmul(act_rel[:, :ff_rows], w_down) + matmul(act_rel[:, ff_rows:], rest_down) + bias_down
    )
    second_sum = normed_one + branch
    output_rows = layer_norm(second_sum, norm_gtwo, norm_stwo)

    def half(value, width, which):
        split = value.reshape(seq_len, -1, 2, width)
        return lax.dynamic_index_in_dim(split, which, axis=2, keepdims=False).reshape(seq_len, -1)

    def pair(value, width):
        return (half(value, width, core), sibling(half(value, width, 1 - core)))

    def both(left, right):
        return outer_sum(left[0], right[0]) + outer_sum(left[1], right[1])

    in_pair = (in_rel, sibling(in_rel))
    context_pair = (context_rel, sibling(context_rel))
    normed_pair = (normed_rel, sibling(normed_rel))
    act_pair = pair(act_rel, part_down)

    def own_sum(parts):
        total = parts[0].astype(jnp.float32)
        for s in range(1, group):
            total = total + to_shard(parts[s], s).astype(jnp.float32)
        return total.astype(jnp.bfloat16)

    def scatter_columns(grad):
        share = lax.psum_scatter(grad.astype(jnp.bfloat16), "chip", scatter_dimension=1, tiled=True)
        share = own_sum(share.reshape(group, rows, -1))
        return lax.all_gather(share, REP, axis=1, tiled=True).astype(jnp.float32)

    grad_rows = cotangent[0].astype(jnp.float32)
    _, norm_two_back = jax.vjp(layer_norm, second_sum, norm_gtwo, norm_stwo)
    grad_second, grad_gtwo, grad_stwo = norm_two_back(grad_rows)
    grad_branch = grad_second.astype(jnp.bfloat16)
    branch_pair = (grad_branch, sibling(grad_branch))
    grad_bdown = column_sum(grad_branch)
    grad_down = both(act_pair, branch_pair).astype(jnp.bfloat16)
    grad_down = lax.psum_scatter(
        grad_down.reshape(group, chips * part_down, model_width),
        "chip",
        scatter_dimension=1,
        tiled=True,
    )
    grad_wdown = lax.all_gather(own_sum(grad_down), REP, axis=0, tiled=True).astype(jnp.float32)
    grad_act = jnp.concatenate(
        [project_back(grad_branch, w_down), project_back(grad_branch, rest_down)], axis=1
    )
    grad_act = roll_right(grad_act, ff_rows)
    _, gelu_back = jax.vjp(partial(jax.nn.gelu, approximate=False), inner)
    grad_inner = gelu_back(grad_act)[0].astype(jnp.bfloat16)
    grad_win = scatter_columns(both(normed_pair, pair(grad_inner, part_in)))
    grad_bin = column_sum(grad_inner)
    back_in = jnp.concatenate(
        [project_back(grad_inner, w_in), project_back(grad_inner, rest_in)], axis=1
    )
    grad_normed = grad_second + roll_right(back_in, rows)
    _, norm_one_back = jax.vjp(layer_norm, first_sum, norm_gone, norm_sone)
    grad_first, grad_gone, grad_sone = norm_one_back(grad_normed)
    grad_attn = grad_first.astype(jnp.bfloat16)
    half_out = both(context_pair, pair(grad_attn, part))
    grad_bout = column_sum(grad_attn)
    grad_context = jnp.concatenate(
        [project_back(grad_attn, own_out), project_back(grad_attn, rest_out)], axis=1
    ).astype(jnp.bfloat16)
    grad_context = roll_right(grad_context, rows).reshape(split_shape)
    grad_query, grad_key, grad_value = attend_back(
        query_heads, key_heads, value_heads, grad_context, allowed, log_totals
    )
    grad_query = grad_query.reshape(-1, model_width)
    grad_key = grad_key.reshape(-1, model_width)
    grad_value = grad_value.reshape(-1, model_width)
    grad_proj = jnp.concatenate([grad_query, grad_key, grad_value], axis=1)
    half_qkv = both(in_pair, pair(grad_proj, part))
    grad_one = scatter_columns(jnp.concatenate([half_qkv, half_out], axis=1))
    back_proj = jnp.concatenate(
        [project_back(grad_proj, own_qkv), project_back(grad_proj, rest_qkv)], axis=1
    )
    grad_input = grad_first + roll_right(back_proj, rows)
    small = (
        jnp.concatenate([column_sum(grad_query), column_sum(grad_value)]),
        grad_bout,
        grad_gone,
        grad_sone,
        grad_bin,
        grad_bdown,
        grad_gtwo,
        grad_stwo,
    )
    small = jnp.concatenate([v.reshape(group, -1) for v in small], axis=1)
    small = lax.psum(small, ALL)
    small = lax.dynamic_index_in_dim(small, own, axis=0, keepdims=False)
    vecs, start = ([], 0)
    for size in sizes:
        vecs.append(small[start : start + size])
        start += size
    return (
        output_rows.astype(jnp.bfloat16).reshape(tokens.shape),
        grad_input.reshape(tokens.shape),
        grad_one[:, :qkv_width],
        vecs[0],
        grad_one[:, qkv_width:],
        vecs[1],
        vecs[2],
        vecs[3],
        grad_win,
        vecs[4],
        grad_wdown,
        vecs[5],
        vecs[6],
        vecs[7],
    )


def solution(mesh):
    reps, group = mesh.devices.shape
    fine = Mesh(mesh.devices.reshape(reps // 2, 2, group), ALL)
    rows = P(ALL, None, None)
    matrix = P("shard", None)
    vector = P("shard")
    in_specs = (
        rows,
        P(ALL, None),
        P(ALL),
        rows,
        matrix,
        vector,
        matrix,
        vector,
        vector,
        vector,
        matrix,
        vector,
        matrix,
        vector,
        vector,
        vector,
    )
    out_specs = (
        rows,
        rows,
        matrix,
        vector,
        matrix,
        vector,
        vector,
        vector,
        matrix,
        vector,
        matrix,
        vector,
        vector,
        vector,
    )
    return jax.shard_map(
        partial(local, reps // 2, group),
        mesh=fine,
        in_specs=in_specs,
        out_specs=out_specs,
        check_vma=False,
    )
```

profile of v0, /device:TPU:0, one launch (start us, length us, event | category | flops | bytes accessed | tf_op | source)
XLA Modules:
  0.0 575.3 jit_solution(13355373292585005239)
XLA Ops:
  15.2 3.1 collective-permute-start.2
  18.3 2.6 collective-permute-start.1
  22.3 5.7 collective-permute-done.2
  28.0 11.1 %collective-permute-done.1 = bf16[272,512]{1,0:T(8,128)(2,1)S(1)} collective-permute-done((bf16[272,512]{1,0:T(8,128)(2,1)S(1)}, bf16[272,512]{1,0:T(8,128)(2,1)S(1)}, u32[]{:S(2)}, u32[]{:S(2)}) %collective-permute-start.1) | collective-permute-done | bytes 278560 | tf_op jit(solution)/shard_map/ppermute | solution.py:130
  41.6 5.8 %collective-permute-start.5 = (bf16[256,512]{1,0:T(8,128)(2,1)S(1)}, bf16[256,512]{1,0:T(8,128)(2,1)S(1)}, u32[]{:S(2)}, u32[]{:S(2)}) collective-permute-start(bf16[256,512]{1,0:T(8,128)(2,1)S(1)} %constant_dynamic-slice_fusion.11), channel_id=1, source_target_pairs={{0,1},{1,2},{2,3},{3,0},{4,5},{5,6},{6,7},{7,4},{8,9},{9,10},{10,1... | collective-permute-start | bytes 786440 | tf_op jit(solution)/shard_map/ppermute | solution.py:130
  47.4 2.3 collective-permute-start.4
  49.8 6.6 %collective-permute-done.5 = bf16[256,512]{1,0:T(8,128)(2,1)S(1)} collective-permute-done((bf16[256,512]{1,0:T(8,128)(2,1)S(1)}, bf16[256,512]{1,0:T(8,128)(2,1)S(1)}, u32[]{:S(2)}, u32[]{:S(2)}) %collective-permute-start.5) | collective-permute-done | bytes 262176 | tf_op jit(solution)/shard_map/ppermute | solution.py:130
  56.4 9.4 %collective-permute-done.4 = bf16[256,512]{1,0:T(8,128)(2,1)S(1)} collective-permute-done((bf16[256,512]{1,0:T(8,128)(2,1)S(1)}, bf16[256,512]{1,0:T(8,128)(2,1)S(1)}, u32[]{:S(2)}, u32[]{:S(2)}) %collective-permute-start.4) | collective-permute-done | bytes 262176 | tf_op jit(solution)/shard_map/ppermute | solution.py:130
  68.6 6.1 %collective-permute-start.8 = (bf16[128,1024]{1,0:T(8,128)(2,1)}, bf16[128,1024]{1,0:T(8,128)(2,1)}, u32[]{:S(2)}, u32[]{:S(2)}) collective-permute-start(bf16[128,1024]{1,0:T(8,128)(2,1)} %constant_dynamic-slice_fusion.10), channel_id=1, source_target_pairs={{0,1},{1,2},{2,3},{3,0},{4,5},{5,6},{6,7},{7,4},{8,9},{9,10},{10,1... | collective-permute-start | bytes 786440 | tf_op jit(solution)/shard_map/ppermute | solution.py:130
  79.7 3.7 collective-permute-done.8
  83.4 10.0 %collective-permute-done.7 = bf16[128,1024]{1,0:T(8,128)(2,1)} collective-permute-done((bf16[128,1024]{1,0:T(8,128)(2,1)}, bf16[128,1024]{1,0:T(8,128)(2,1)}, u32[]{:S(2)}, u32[]{:S(2)}) %collective-permute-start.7) | collective-permute-done | bytes 262176 | tf_op jit(solution)/shard_map/ppermute | solution.py:130
  100.2 4.8 fusion.18
  109.8 2.3 copy.68
  114.8 9.4 %fusion.82 = (f32[16,512]{1,0:T(8,128)S(1)}, f32[16,512,512]{1,2,0:T(8,128)}) fusion(bf16[512,16,64]{0,2,1:T(8,128)(2,1)} %bitcast.174, bf16[512,16,64]{0,2,1:T(8,128)(2,1)S(1)} %bitcast.172, pred[512,512]{0,1:T(8,128)(4,1)S(1)} %compare_and_fusion), kind=kOutput, calls=%fused_computation.211 | convolution fusion | flops 549445632 | bytes 19169280 | tf_op jit(solution)/shard_map/qhd,khd->hqk/dot_general | solution.py:49
  124.3 8.4 %fusion = f32[16,512]{1,0:T(8,128)S(1)} fusion(f32[16,512,512]{1,2,0:T(8,128)} %get-tuple-element.65, f32[16,512]{1,0:T(8,128)S(1)} %get-tuple-element.64), kind=kLoop, calls=%fused_computation.10 | loop fusion | flops 8380416 | bytes 16842752 | tf_op jit(solution)/shard_map/reduce_sum | solution.py:55
  132.6 7.7 %fusion.42 = bf16[16,64,512]{2,1,0:T(8,128)(2,1)S(1)} fusion(bf16[512,16,64]{0,2,1:T(8,128)(2,1)S(1)} %bitcast.184, f32[16,512,512]{1,2,0:T(8,128)} %get-tuple-element.65, f32[16,512]{1,0:T(8,128)S(1)} %fusion, f32[16,512]{1,0:T(8,128)S(1)} %get-tuple-element.64), kind=kOutput, calls=%fused_computation.115 | convolution fusion | flops 549978112 | bytes 18939904 | tf_op jit(solution)/shard_map/hqk,khd->qhd/dot_general | solution.py:57
  140.3 2.8 fusion.55
  143.2 2.8 fusion.47
  149.9 4.6 fusion.67
  154.5 24.8 %multiply_convert_fusion.1 = (bf16[512,4096]{1,0:T(8,128)(2,1)S(1)}, f32[512,4096]{1,0:T(8,128)}) fusion(f32[4096]{0:T(1024)S(1)} %bitcast.218, f32[512,4096]{1,0:T(8,128)} %fusion.67, bf16[768,4096]{1,0:T(8,128)(2,1)} %all-gather.9.cloned.1.call-done, bf16[512,1024]{1,0:T(8,128)(2,1)S(1)} %fusion.54), kind=kOutput, calls=%fused_computation.25 | convolution fusion | flops 3361734656 | bytes 28065792 | tf_op jit(solution)/shard_map/dot_general | solution.py:21
  179.2 2.5 fusion.15
  183.7 2.6 fusion.57
  186.3 3.7 all-gather.11.cloned.1.call-done
  190.0 8.7 %fusion.84 = (f32[512]{0:T(512)S(1)}, f32[512,1024]{1,0:T(8,128)S(1)}) fusion(f32[1024]{0:T(1024)S(1)} %bitcast.220, f32[512,1024]{1,0:T(8,128)} %fusion.57, bf16[3072,1024]{1,0:T(8,128)(2,1)} %bitcast.229, bf16[512,4096]{1,0:T(8,128)(2,1)} %copy-done.6, f32[1024]{0:T(1024)S(1)} %bitcast.214, f32[1024]{0:T(1024)S(1)} %bitcast.207, f32[512]{0:T(512)S(1)} %fusion.72, ...), kind=kOutput, calls=%fused_computation.213 | convolution fusion | flops 3225419264 | bytes 15747072 | tf_op jit(solution)/shard_map/dot_general | solution.py:21
  202.2 6.1 %fusion.86 = f32[512,3072]{1,0:T(8,128)S(1)} fusion(bf16[512,1024]{1,0:T(8,128)(2,1)S(1)} %get-tuple-element.20, bf16[3072,1024]{1,0:T(8,128)(2,1)} %bitcast.230), kind=kOutput, calls=%fused_computation.215 | convolution fusion | flops 3221225472 | bytes 13631488 | tf_op jit(solution)/shard_map/dot_general | solution.py:25
  209.7 23.1 %convert_reduce_fusion = (f32[4096]{0:T(1024)S(1)}, bf16[512,4096]{1,0:T(8,128)(2,1)S(1)}) fusion(f32[512,4096]{1,0:T(8,128)S(1)} %bitcast.179, s32[]{:T(128)S(6)} %select_n.73, f32[512,3072]{1,0:T(8,128)S(1)} %fusion.86, f32[512,1024]{1,0:T(8,128)S(1)} %fusion.85), kind=kLoop, calls=%fused_computation.22 | loop fusion | flops 161476608 | bytes 20987908 | tf_op jit(solution)/shard_map/reduce_sum | solution.py:37
  234.3 5.9 %fusion.88 = f32[512,768]{1,0:T(8,128)S(1)} fusion(bf16[512,4096]{1,0:T(8,128)(2,1)S(1)} %get-tuple-element.22, bf16[768,4096]{1,0:T(8,128)(2,1)} %all-gather.9.cloned.1.call-done), kind=kOutput, calls=%fused_computation.217 | convolution fusion | flops 3221225472 | bytes 12058624 | tf_op jit(solution)/shard_map/dot_general | solution.py:25
  245.1 2.4 convolution_convert_fusion
  248.7 8.6 %convert_reduce_fusion.4 = (f32[16,64]{1,0:T(8,128)S(1)}, bf16[16,64,512]{2,1,0:T(8,128)(2,1)S(1)}) fusion(bf16[512,16,64]{0,2,1:T(8,128)(2,1)S(1)} %bitcast.176, f32[16,512,512]{1,2,0:T(8,128)} %get-tuple-element.65, f32[16,512]{1,0:T(8,128)S(1)} %log_add_fusion), kind=kOutput, calls=%fused_computation.100 | convolution fusion | flops 546831360 | bytes 18911232 | tf_op jit(solution)/shard_map/hqk,qhd->khd/dot_general | solution.py:85
  257.4 11.4 %multiply_reduce_fusion = (f32[16,512]{1,0:T(8,128)S(1)}, f32[16,512,512]{1,2,0:T(8,128)}) fusion(f32[16,512,512]{1,2,0:T(8,128)} %get-tuple-element.65, f32[16,512]{1,0:T(8,128)S(1)} %log_add_fusion, bf16[512,16,64]{0,2,1:T(8,128)(2,1)S(1)} %bitcast.177, bf16[512,16,64]{0,2,1:T(8,128)(2,1)S(1)} %bitcast.185), kind=kOutput, calls=%fused_computation.5 | convolution fusion | flops 549445632 | bytes 35717120 | tf_op jit(solution)/shard_map/qhd,khd->hqk/dot_general | solution.py:71
  268.8 12.0 %multiply_convert_fusion = bf16[16,512,512]{1,2,0:T(8,128)(2,1)S(1)} fusion(f32[16,512,512]{1,2,0:T(8,128)} %get-tuple-element.73, f32[16,512,512]{1,2,0:T(8,128)} %get-tuple-element.65, f32[16,512]{1,0:T(8,128)S(1)} %get-tuple-element.72, f32[16,512]{1,0:T(8,128)S(1)} %log_add_fusion), kind=kLoop, calls=%fused_computation.4 | loop fusion | flops 16777216 | bytes 42008576 | tf_op jit(solution)/shard_map/convert_element_type | solution.py:77
  280.8 2.6 multiply_convert_fusion.2
  290.0 2.2 constant_dynamic-slice_fusion.6
  294.5 3.1 fusion.89
  299.6 3.6 add_convert_fusion.3
  303.2 2.7 pad_maximum_fusion
  306.0 8.1 %reshape.403 = bf16[512,4,2,512]{3,2,1,0:T(2,128)(2,1)} reshape(bf16[512,4096]{1,0:T(8,128)(2,1)} %copy-done.7) | data formatting | bytes 8388608 | tf_op jit(solution)/shard_map/reshape | solution.py:209
  314.0 11.3 %constant_dynamic-slice_fusion.3 = (bf16[512,4,1,512]{3,2,1,0:T(2,128)(2,1)}, bf16[512,4,1,512]{3,2,1,0:T(2,128)(2,1)}) fusion(bf16[512,4,2,512]{3,2,1,0:T(2,128)(2,1)} %reshape.403, s32[]{:T(128)S(6)} %select_n.76, s32[]{:T(128)S(6)} %select_n.75), kind=kLoop, calls=%fused_computation.175 | loop fusion | bytes 8388616 | tf_op jit(solution)/shard_map/jit(dynamic_index_in_dim)/dynamic_slice | solution.py:210
  325.3 9.1 %copy.100 = bf16[512,4,1,512]{0,3,1,2:T(8,128)(2,1)S(1)} copy(bf16[512,4,1,512]{3,2,1,0:T(2,128)(2,1)} %get-tuple-element.34) | data formatting | bytes 4194304
  334.9 10.5 %copy.99 = bf16[512,4,1,512]{0,3,1,2:T(8,128)(2,1)} copy(bf16[512,4,1,512]{3,2,1,0:T(2,128)(2,1)} %get-tuple-element.35) | data formatting | bytes 4194304
  345.5 4.3 fusion.90
  349.8 6.3 %add_convert_fusion.1 = bf16[1024,2048]{1,0:T(8,128)(2,1)} fusion(f32[1024,2048]{1,0:T(8,128)S(1)} %fusion.90, bf16[512,1024]{1,0:T(8,128)(2,1)} %collective-permute-done.16, bf16[512,2048]{0,1:T(8,128)(2,1)} %collective-permute-done.17), kind=kOutput, calls=%fused_computation.21 | convolution fusion | flops 2151677952 | bytes 15728640 | tf_op jit(solution)/shard_map/dot_general | solution.py:31
  356.2 6.5 %copy.88 = bf16[512,4096]{0,1:T(8,128)(2,1)} copy(bf16[512,4096]{1,0:T(8,128)(2,1)} %copy-done.6) | data formatting | bytes 8388608 | tf_op jit(solution)/shard_map/dynamic_slice | solution.py:140
  362.7 2.6 constant_dynamic-slice_fusion.1
  365.9 2.4 fusion.91
  368.4 2.7 collective-permute-done.22
  371.1 4.5 add_convert_fusion
  376.9 3.8 collective-permute-start.15
  381.8 5.7 collective-permute-done.15
  387.5 16.6 %collective-permute-done.14 = bf16[256,512]{1,0:T(8,128)(2,1)S(1)} collective-permute-done((bf16[256,512]{1,0:T(8,128)(2,1)S(1)}, bf16[256,512]{1,0:T(8,128)(2,1)S(1)}, u32[]{:S(2)}, u32[]{:S(2)}) %collective-permute-start.14) | collective-permute-done | bytes 262176 | tf_op jit(solution)/shard_map/ppermute | solution.py:133
  405.9 9.9 %reduce-scatter.6.cloned.1.call-done = bf16[1024,512]{1,0:T(8,128)(2,1)} async-done(((bf16[1024,2048]{1,0:T(8,128)(2,1)}), bf16[1024,512]{1,0:T(8,128)(2,1)}) %reduce-scatter.6.cloned.1.call-update) | async-done | bytes 1048592 | tf_op jit(solution)/shard_map/reduce_scatter | solution.py:230
  417.0 3.4 collective-permute-start.20
  421.5 5.7 collective-permute-done.20
  427.2 15.7 %collective-permute-done.19 = bf16[256,512]{1,0:T(8,128)(2,1)S(1)} collective-permute-done((bf16[256,512]{1,0:T(8,128)(2,1)S(1)}, bf16[256,512]{1,0:T(8,128)(2,1)S(1)}, u32[]{:S(2)}, u32[]{:S(2)}) %collective-permute-start.19) | collective-permute-done | bytes 262176 | tf_op jit(solution)/shard_map/ppermute | solution.py:133
  444.8 27.2 %reduce-scatter.8.cloned.1.call-done = bf16[4,128,1024]{2,1,0:T(8,128)(2,1)} async-done(((bf16[4,512,1024]{2,1,0:T(8,128)(2,1)}), bf16[4,128,1024]{2,1,0:T(8,128)(2,1)}) %reduce-scatter.8.cloned.1.call-update) | async-done | bytes 1048592 | tf_op jit(solution)/shard_map/reduce_scatter | solution.py:241
  473.2 3.4 collective-permute-start.25
  477.7 5.6 collective-permute-done.25
  483.3 15.8 %collective-permute-done.24 = bf16[128,1024]{1,0:T(8,128)(2,1)S(1)} collective-permute-done((bf16[128,1024]{1,0:T(8,128)(2,1)S(1)}, bf16[128,1024]{1,0:T(8,128)(2,1)S(1)}, u32[]{:S(2)}, u32[]{:S(2)}) %collective-permute-start.24) | collective-permute-done | bytes 262176 | tf_op jit(solution)/shard_map/ppermute | solution.py:133
  501.4 40.2 %psum.7 = f32[4,3072]{1,0:T(4,128)S(1)} all-reduce(f32[4,3072]{1,0:T(4,128)S(1)} %constant_dynamic-update-slice_fusion), channel_id=1, replica_groups=mesh['chip'=4,'core'=2,'shard'=4] {'chip','core','shard'}, use_global_device_ids=true, to_apply=%region_21.22 | all-reduce | flops 12288 | bytes 98304 | tf_op jit(solution)/shard_map/psum | solution.py:293
  543.5 3.0 fusion.49
  546.6 5.1 fusion.16
  553.7 3.6 slice.278
  558.4 4.3 convert_element_type.279
  564.4 4.1 convert_element_type.287
  (254 shorter events, 82.9 us)
Async XLA Ops:
  7.2 34.3 %copy-start = (bf16[256,4096]{1,0:T(8,128)(2,1)S(1)}, bf16[256,4096]{1,0:T(8,128)(2,1)}, u32[]{:S(2)}) copy-start(bf16[256,4096]{1,0:T(8,128)(2,1)} %param.26) | copy-start | bytes 6291460
  7.2 93.0 %all-gather.7.cloned.1.call-start = ((), (), s32[]{:S(2)}) async-start(), calls=%async_computation.3 | async-start | bytes 7077888 | tf_op jit(solution)/shard_map/all_gather | solution.py:165
  15.2 62.5 %copy-start.17 = (bf16[1,512,1024]{2,1,0:T(8,128)(2,1)S(1)}, bf16[1,512,1024]{2,1,0:T(8,128)(2,1)}, u32[]{:S(2)}) copy-start(bf16[1,512,1024]{2,1,0:T(8,128)(2,1)} %param.16) | copy-start | bytes 3145732
  15.2 12.7 %collective-permute-start.2 = (bf16[272,512]{1,0:T(8,128)(2,1)S(1)}, bf16[272,512]{1,0:T(8,128)(2,1)S(1)}, u32[]{:S(2)}, u32[]{:S(2)}) collective-permute-start(bf16[272,512]{1,0:T(8,128)(2,1)S(1)} %pad_maximum_fusion.8), channel_id=1, source_target_pairs={{0,1},{1,2},{2,3},{3,0},{4,5},{5,6},{6,7},{7,4},{8,9},{9,10},{10,1... | collective-permute-start | bytes 835592 | tf_op jit(solution)/shard_map/ppermute | solution.py:130
  18.3 20.8 %collective-permute-start.1 = (bf16[272,512]{1,0:T(8,128)(2,1)S(1)}, bf16[272,512]{1,0:T(8,128)(2,1)S(1)}, u32[]{:S(2)}, u32[]{:S(2)}) collective-permute-start(bf16[272,512]{1,0:T(8,128)(2,1)S(1)} %pad_maximum_fusion.8), channel_id=1, source_target_pairs={{0,2},{1,3},{2,0},{3,1},{4,6},{5,7},{6,4},{7,5},{8,10},{9,11},{10,... | collective-permute-start | bytes 835592 | tf_op jit(solution)/shard_map/ppermute | solution.py:130
  20.9 18.2 %collective-permute-start = (bf16[272,512]{1,0:T(8,128)(2,1)S(1)}, bf16[272,512]{1,0:T(8,128)(2,1)S(1)}, u32[]{:S(2)}, u32[]{:S(2)}) collective-permute-start(bf16[272,512]{1,0:T(8,128)(2,1)S(1)} %pad_maximum_fusion.8), channel_id=1, source_target_pairs={{0,3},{1,0},{2,1},{3,2},{4,7},{5,4},{6,5},{7,6},{8,11},{9,8},{10,9... | collective-permute-start | bytes 835592 | tf_op jit(solution)/shard_map/ppermute | solution.py:130
  28.0 11.1 %copy-start.33 = (bf16[272,512]{1,0:T(8,128)(2,1)}, bf16[272,512]{1,0:T(8,128)(2,1)S(1)}, u32[]{:S(2)}) copy-start(bf16[272,512]{1,0:T(8,128)(2,1)S(1)} %collective-permute-done.2) | copy-start | bytes 835588
  39.1 40.3 %copy-start.40 = (s32[1,512]{1,0:T(1,128)S(1)}, s32[1,512]{1,0:T(1,128)}, u32[]{:S(2)}) copy-start(s32[1,512]{1,0:T(1,128)} %param.17) | copy-start | bytes 6148
  41.5 113.0 %all-gather.9.cloned.1.call-start = ((), (), s32[]{:S(2)}) async-start(), calls=%async_computation.4 | async-start | bytes 7077888 | tf_op jit(solution)/shard_map/all_gather | solution.py:168
  41.6 14.9 %collective-permute-start.5 = (bf16[256,512]{1,0:T(8,128)(2,1)S(1)}, bf16[256,512]{1,0:T(8,128)(2,1)S(1)}, u32[]{:S(2)}, u32[]{:S(2)}) collective-permute-start(bf16[256,512]{1,0:T(8,128)(2,1)S(1)} %constant_dynamic-slice_fusion.11), channel_id=1, source_target_pairs={{0,1},{1,2},{2,3},{3,0},{4,5},{5,6},{6,7},{7,4},{8,9},{9,10},{10,1... | collective-permute-start | bytes 786440 | tf_op jit(solution)/shard_map/ppermute | solution.py:130
  47.4 18.5 %collective-permute-start.4 = (bf16[256,512]{1,0:T(8,128)(2,1)S(1)}, bf16[256,512]{1,0:T(8,128)(2,1)S(1)}, u32[]{:S(2)}, u32[]{:S(2)}) collective-permute-start(bf16[256,512]{1,0:T(8,128)(2,1)S(1)} %constant_dynamic-slice_fusion.11), channel_id=1, source_target_pairs={{0,2},{1,3},{2,0},{3,1},{4,6},{5,7},{6,4},{7,5},{8,10},{9,11},{10,... | collective-permute-start | bytes 786440 | tf_op jit(solution)/shard_map/ppermute | solution.py:130
  49.6 16.2 %collective-permute-start.3 = (bf16[256,512]{1,0:T(8,128)(2,1)S(1)}, bf16[256,512]{1,0:T(8,128)(2,1)S(1)}, u32[]{:S(2)}, u32[]{:S(2)}) collective-permute-start(bf16[256,512]{1,0:T(8,128)(2,1)S(1)} %constant_dynamic-slice_fusion.11), channel_id=1, source_target_pairs={{0,3},{1,0},{2,1},{3,2},{4,7},{5,4},{6,5},{7,6},{8,11},{9,8},{10,9... | collective-permute-start | bytes 786440 | tf_op jit(solution)/shard_map/ppermute | solution.py:130
  66.8 123.2 %all-gather.11.cloned.1.call-start = ((), (), s32[]{:S(2)}) async-start(), calls=%async_computation.5 | async-start | bytes 7077888 | tf_op jit(solution)/shard_map/all_gather | solution.py:169
  68.6 14.8 %collective-permute-start.8 = (bf16[128,1024]{1,0:T(8,128)(2,1)}, bf16[128,1024]{1,0:T(8,128)(2,1)}, u32[]{:S(2)}, u32[]{:S(2)}) collective-permute-start(bf16[128,1024]{1,0:T(8,128)(2,1)} %constant_dynamic-slice_fusion.10), channel_id=1, source_target_pairs={{0,1},{1,2},{2,3},{3,0},{4,5},{5,6},{6,7},{7,4},{8,9},{9,10},{10,1... | collective-permute-start | bytes 786440 | tf_op jit(solution)/shard_map/ppermute | solution.py:130
  74.7 18.7 %collective-permute-start.7 = (bf16[128,1024]{1,0:T(8,128)(2,1)}, bf16[128,1024]{1,0:T(8,128)(2,1)}, u32[]{:S(2)}, u32[]{:S(2)}) collective-permute-start(bf16[128,1024]{1,0:T(8,128)(2,1)} %constant_dynamic-slice_fusion.10), channel_id=1, source_target_pairs={{0,2},{1,3},{2,0},{3,1},{4,6},{5,7},{6,4},{7,5},{8,10},{9,11},{10,... | collective-permute-start | bytes 786440 | tf_op jit(solution)/shard_map/ppermute | solution.py:130
  76.3 17.1 %collective-permute-start.6 = (bf16[128,1024]{1,0:T(8,128)(2,1)}, bf16[128,1024]{1,0:T(8,128)(2,1)}, u32[]{:S(2)}, u32[]{:S(2)}) collective-permute-start(bf16[128,1024]{1,0:T(8,128)(2,1)} %constant_dynamic-slice_fusion.10), channel_id=1, source_target_pairs={{0,3},{1,0},{2,1},{3,2},{4,7},{5,4},{6,5},{7,6},{8,11},{9,8},{10,9... | collective-permute-start | bytes 786440 | tf_op jit(solution)/shard_map/ppermute | solution.py:130
  95.5 280.1 %reduce-scatter.4.cloned.1.call-start = ((), (), s32[]{:S(2)}) async-start(), calls=%async_computation.6 | async-start | bytes 5242880 | tf_op jit(solution)/shard_map/reduce_scatter | solution.py:230
  100.2 4.8 copy-start.16
  114.8 9.4 %copy-start.8 = (bf16[512,1024]{0,1:T(8,128)(2,1)}, bf16[512,1024]{0,1:T(8,128)(2,1)S(1)}, u32[]{:S(2)}) copy-start(bf16[512,1024]{0,1:T(8,128)(2,1)S(1)} %copy.70) | copy-start | bytes 3145732
  124.3 8.4 %copy-start.19 = (bf16[512,1024]{0,1:T(8,128)(2,1)S(1)}, bf16[512,1024]{0,1:T(8,128)(2,1)}, u32[]{:S(2)}) copy-start(bf16[512,1024]{0,1:T(8,128)(2,1)} %copy.68) | copy-start | bytes 3145732
  149.9 4.6 copy-start.29
  179.2 4.5 copy-start.37
  190.0 9.1 %copy-start.11 = (bf16[1,512,1024]{2,1,0:T(8,128)(2,1)S(1)}, bf16[1,512,1024]{2,1,0:T(8,128)(2,1)}, u32[]{:S(2)}) copy-start(bf16[1,512,1024]{2,1,0:T(8,128)(2,1)} %param.19) | copy-start | bytes 3145732
  190.0 9.1 %copy-start.36 = (f32[1,2,4,128]{3,1,2,0:T(2,128)S(1)}, f32[1,2,4,128]{3,1,2,0:T(2,128)}, u32[]{:S(2)}) copy-start(f32[1,2,4,128]{3,1,2,0:T(2,128)} %copy.111) | copy-start | bytes 12292
  202.2 6.2 %copy-start.31 = (bf16[512,1024]{1,0:T(8,128)(2,1)}, bf16[512,1024]{1,0:T(8,128)(2,1)S(1)}, u32[]{:S(2)}) copy-start(bf16[512,1024]{1,0:T(8,128)(2,1)S(1)} %get-tuple-element.20) | copy-start | bytes 3145732
  202.2 7.5 %slice-start = ((s8[8388608]{0:T(1024)(128)(4,1)}), s8[4194304]{0:T(1024)(128)(4,1)S(1)}, s32[]{:S(2)}) async-start(s8[8388608]{0:T(1024)(128)(4,1)} %bitcast.178), calls=%async_computation.12 | async-start | bytes 8388608
  202.2 6.2 %copy-start.38 = (bf16[1024,1024]{1,0:T(8,128)(2,1)S(1)}, bf16[1024,1024]{1,0:T(8,128)(2,1)}, u32[]{:S(2)}) copy-start(bf16[1024,1024]{1,0:T(8,128)(2,1)} %param.28) | copy-start | bytes 6291460
  202.2 7.5 %slice-start.1 = ((s8[8388608]{0:T(1024)(128)(4,1)}), s8[4194304]{0:T(1024)(128)(4,1)S(1)}, s32[]{:S(2)}) async-start(s8[8388608]{0:T(1024)(128)(4,1)} %bitcast.178), calls=%async_computation.13 | async-start | bytes 8388608
  232.8 7.4 %copy-start.7 = (bf16[512,4096]{1,0:T(8,128)(2,1)}, bf16[512,4096]{1,0:T(8,128)(2,1)S(1)}, u32[]{:S(2)}) copy-start(bf16[512,4096]{1,0:T(8,128)(2,1)S(1)} %get-tuple-element.22) | copy-start | bytes 12582916
  234.3 5.9 %copy-start.3 = (f32[512,1024]{1,0:T(8,128)S(1)}, f32[512,1024]{1,0:T(8,128)}, u32[]{:S(2)}) copy-start(f32[512,1024]{1,0:T(8,128)} %copy-done.2) | copy-start | bytes 6291460
  244.4 3.1 copy-start.26
  248.7 8.6 %copy-start.20 = (bf16[512,1024]{0,1:T(8,128)(2,1)S(1)}, bf16[512,1024]{0,1:T(8,128)(2,1)}, u32[]{:S(2)}) copy-start(bf16[512,1024]{0,1:T(8,128)(2,1)} %copy.68) | copy-start | bytes 3145732
  257.4 27.5 %copy-start.21 = (bf16[16,64,512]{2,1,0:T(8,128)(2,1)}, bf16[16,64,512]{2,1,0:T(8,128)(2,1)S(1)}, u32[]{:S(2)}) copy-start(bf16[16,64,512]{2,1,0:T(8,128)(2,1)S(1)} %get-tuple-element.75) | copy-start | bytes 3145732
  268.8 12.0 %copy-start.10 = (bf16[512,1024]{0,1:T(8,128)(2,1)S(1)}, bf16[512,1024]{0,1:T(8,128)(2,1)}, u32[]{:S(2)}) copy-start(bf16[512,1024]{0,1:T(8,128)(2,1)} %copy.69) | copy-start | bytes 3145732
  287.3 12.2 %collective-permute-start.10 = (bf16[512,1536]{0,1:T(8,128)(2,1)}, bf16[512,1536]{0,1:T(8,128)(2,1)}, u32[]{:S(2)}, u32[]{:S(2)}) collective-permute-start(bf16[512,1536]{0,1:T(8,128)(2,1)} %bitcast.26), channel_id=1, source_target_pairs={{0,4},{4,0},{1,5},{5,1},{2,6},{6,2},{3,7},{7,3},{8,12},{12,8},{9,1... | collective-permute-start | bytes 4718600 | tf_op jit(solution)/shard_map/ppermute | solution.py:136
  287.6 10.0 %collective-permute-start.11 = (bf16[512,1024]{0,1:T(8,128)(2,1)}, bf16[512,1024]{0,1:T(8,128)(2,1)}, u32[]{:S(2)}, u32[]{:S(2)}) collective-permute-start(bf16[512,1024]{0,1:T(8,128)(2,1)} %fusion.55), channel_id=1, source_target_pairs={{0,4},{4,0},{1,5},{5,1},{2,6},{6,2},{3,7},{7,3},{8,12},{12,8},{9,1... | collective-permute-start | bytes 3145736 | tf_op jit(solution)/shard_map/ppermute | solution.py:136
  287.8 11.7 %collective-permute-start.9 = (bf16[512,1024]{1,0:T(8,128)(2,1)}, bf16[512,1024]{1,0:T(8,128)(2,1)}, u32[]{:S(2)}, u32[]{:S(2)}) collective-permute-start(bf16[512,1024]{1,0:T(8,128)(2,1)} %fusion.56), channel_id=1, source_target_pairs={{0,4},{4,0},{1,5},{5,1},{2,6},{6,2},{3,7},{7,3},{8,12},{12,8},{9,1... | collective-permute-start | bytes 3145736 | tf_op jit(solution)/shard_map/ppermute | solution.py:136
  289.9 4.6 copy-start.30
  292.3 5.3 collective-permute-start.12
  305.9 110.0 %reduce-scatter.6.cloned.1.call-start = ((), (), s32[]{:S(2)}) async-start(), calls=%async_computation.8 | async-start | bytes 5242880 | tf_op jit(solution)/shard_map/reduce_scatter | solution.py:230
  334.4 15.5 %collective-permute-start.17 = (bf16[512,2048]{0,1:T(8,128)(2,1)S(1)}, bf16[512,2048]{0,1:T(8,128)(2,1)}, u32[]{:S(2)}, u32[]{:S(2)}) collective-permute-start(bf16[512,2048]{0,1:T(8,128)(2,1)S(1)} %bitcast.193), channel_id=1, source_target_pairs={{0,4},{4,0},{1,5},{5,1},{2,6},{6,2},{3,7},{7,3},{8,12},{12,8},{9,1... | collective-permute-start | bytes 6291464 | tf_op jit(solution)/shard_map/ppermute | solution.py:136
  334.7 15.1 %collective-permute-start.16 = (bf16[512,1024]{1,0:T(8,128)(2,1)}, bf16[512,1024]{1,0:T(8,128)(2,1)}, u32[]{:S(2)}, u32[]{:S(2)}) collective-permute-start(bf16[512,1024]{1,0:T(8,128)(2,1)} %copy-done.29), channel_id=1, source_target_pairs={{0,4},{4,0},{1,5},{5,1},{2,6},{6,2},{3,7},{7,3},{8,12},{12,8},{9,1... | collective-permute-start | bytes 3145736 | tf_op jit(solution)/shard_map/ppermute | solution.py:136
  356.1 115.9 %reduce-scatter.8.cloned.1.call-start = ((), (), s32[]{:S(2)}) async-start(), calls=%async_computation.10 | async-start | bytes 5242880 | tf_op jit(solution)/shard_map/reduce_scatter | solution.py:241
  362.7 3.1 copy-start.32
  365.3 5.7 collective-permute-start.21
  365.8 5.3 collective-permute-start.22
  375.6 178.2 %all-gather.13.cloned.1.call-start = ((), (), s32[]{:S(2)}) async-start(), calls=%async_computation.7 | async-start | bytes 2359296 | tf_op jit(solution)/shard_map/all_gather | solution.py:232
  376.9 10.6 %collective-permute-start.15 = (bf16[256,512]{1,0:T(8,128)(2,1)S(1)}, bf16[256,512]{1,0:T(8,128)(2,1)S(1)}, u32[]{:S(2)}, u32[]{:S(2)}) collective-permute-start(bf16[256,512]{1,0:T(8,128)(2,1)S(1)} %get-tuple-element.46), channel_id=1, source_target_pairs={{0,3},{1,0},{2,1},{3,2},{4,7},{5,4},{6,5},{7,6},{8,11},{9,8},{10,9... | collective-permute-start | bytes 786440 | tf_op jit(solution)/shard_map/ppermute | solution.py:133
  380.7 23.3 %collective-permute-start.14 = (bf16[256,512]{1,0:T(8,128)(2,1)S(1)}, bf16[256,512]{1,0:T(8,128)(2,1)S(1)}, u32[]{:S(2)}, u32[]{:S(2)}) collective-permute-start(bf16[256,512]{1,0:T(8,128)(2,1)S(1)} %get-tuple-element.47), channel_id=1, source_target_pairs={{0,2},{1,3},{2,0},{3,1},{4,6},{5,7},{6,4},{7,5},{8,10},{9,11},{10,... | collective-permute-start | bytes 786440 | tf_op jit(solution)/shard_map/ppermute | solution.py:133
  380.9 23.2 %collective-permute-start.13 = (bf16[256,512]{1,0:T(8,128)(2,1)S(1)}, bf16[256,512]{1,0:T(8,128)(2,1)S(1)}, u32[]{:S(2)}, u32[]{:S(2)}) collective-permute-start(bf16[256,512]{1,0:T(8,128)(2,1)S(1)} %get-tuple-element.45), channel_id=1, source_target_pairs={{0,1},{1,2},{2,3},{3,0},{4,5},{5,6},{6,7},{7,4},{8,9},{9,10},{10,1... | collective-permute-start | bytes 786440 | tf_op jit(solution)/shard_map/ppermute | solution.py:133
  405.9 137.6 %copy-start.14 = (bf16[16,64,512]{2,1,0:T(8,128)(2,1)S(1)}, bf16[16,64,512]{2,1,0:T(8,128)(2,1)}, u32[]{:S(2)}) copy-start(bf16[16,64,512]{2,1,0:T(8,128)(2,1)} %copy-done.13) | copy-start | bytes 3145732
  405.9 137.6 %copy-start.22 = (bf16[16,64,512]{2,1,0:T(8,128)(2,1)S(1)}, bf16[16,64,512]{2,1,0:T(8,128)(2,1)}, u32[]{:S(2)}) copy-start(bf16[16,64,512]{2,1,0:T(8,128)(2,1)} %copy-done.21) | copy-start | bytes 3145732
  405.9 152.5 %all-gather.15.cloned.1.call-start = ((), (), s32[]{:S(2)}) async-start(), calls=%async_computation.9 | async-start | bytes 2359296 | tf_op jit(solution)/shard_map/all_gather | solution.py:232
  417.0 10.1 %collective-permute-start.20 = (bf16[256,512]{1,0:T(8,128)(2,1)S(1)}, bf16[256,512]{1,0:T(8,128)(2,1)S(1)}, u32[]{:S(2)}, u32[]{:S(2)}) collective-permute-start(bf16[256,512]{1,0:T(8,128)(2,1)S(1)} %get-tuple-element.43), channel_id=1, source_target_pairs={{0,3},{1,0},{2,1},{3,2},{4,7},{5,4},{6,5},{7,6},{8,11},{9,8},{10,9... | collective-permute-start | bytes 786440 | tf_op jit(solution)/shard_map/ppermute | solution.py:133
  420.4 22.5 %collective-permute-start.19 = (bf16[256,512]{1,0:T(8,128)(2,1)S(1)}, bf16[256,512]{1,0:T(8,128)(2,1)S(1)}, u32[]{:S(2)}, u32[]{:S(2)}) collective-permute-start(bf16[256,512]{1,0:T(8,128)(2,1)S(1)} %get-tuple-element.44), channel_id=1, source_target_pairs={{0,2},{1,3},{2,0},{3,1},{4,6},{5,7},{6,4},{7,5},{8,10},{9,11},{10,... | collective-permute-start | bytes 786440 | tf_op jit(solution)/shard_map/ppermute | solution.py:133
  420.4 22.5 %collective-permute-start.18 = (bf16[256,512]{1,0:T(8,128)(2,1)S(1)}, bf16[256,512]{1,0:T(8,128)(2,1)S(1)}, u32[]{:S(2)}, u32[]{:S(2)}) collective-permute-start(bf16[256,512]{1,0:T(8,128)(2,1)S(1)} %get-tuple-element.42), channel_id=1, source_target_pairs={{0,1},{1,2},{2,3},{3,0},{4,5},{5,6},{6,7},{7,4},{8,9},{9,10},{10,1... | collective-permute-start | bytes 786440 | tf_op jit(solution)/shard_map/ppermute | solution.py:133
  444.7 119.7 %all-gather.17.cloned.1.call-start = ((), (), s32[]{:S(2)}) async-start(), calls=%async_computation.11 | async-start | bytes 2359296 | tf_op jit(solution)/shard_map/all_gather | solution.py:247
  473.2 10.1 %collective-permute-start.25 = (bf16[128,1024]{1,0:T(8,128)(2,1)S(1)}, bf16[128,1024]{1,0:T(8,128)(2,1)S(1)}, u32[]{:S(2)}, u32[]{:S(2)}) collective-permute-start(bf16[128,1024]{1,0:T(8,128)(2,1)S(1)} %get-tuple-element.40), channel_id=1, source_target_pairs={{0,3},{1,0},{2,1},{3,2},{4,7},{5,4},{6,5},{7,6},{8,11},{9,8},{10,9... | collective-permute-start | bytes 786440 | tf_op jit(solution)/shard_map/ppermute | solution.py:133
  476.5 22.5 %collective-permute-start.24 = (bf16[128,1024]{1,0:T(8,128)(2,1)S(1)}, bf16[128,1024]{1,0:T(8,128)(2,1)S(1)}, u32[]{:S(2)}, u32[]{:S(2)}) collective-permute-start(bf16[128,1024]{1,0:T(8,128)(2,1)S(1)} %get-tuple-element.41), channel_id=1, source_target_pairs={{0,2},{1,3},{2,0},{3,1},{4,6},{5,7},{6,4},{7,5},{8,10},{9,11},{10,... | collective-permute-start | bytes 786440 | tf_op jit(solution)/shard_map/ppermute | solution.py:133
  476.5 22.5 %collective-permute-start.23 = (bf16[128,1024]{1,0:T(8,128)(2,1)S(1)}, bf16[128,1024]{1,0:T(8,128)(2,1)S(1)}, u32[]{:S(2)}, u32[]{:S(2)}) collective-permute-start(bf16[128,1024]{1,0:T(8,128)(2,1)S(1)} %get-tuple-element.39), channel_id=1, source_target_pairs={{0,1},{1,2},{2,3},{3,0},{4,5},{5,6},{6,7},{7,4},{8,9},{9,10},{10,1... | collective-permute-start | bytes 786440 | tf_op jit(solution)/shard_map/ppermute | solution.py:133
  543.5 3.0 copy-start.23
  546.6 5.2 copy-start.5
  553.7 3.6 copy-start.12
  558.4 10.0 %copy-start.1 = (bf16[256,4096]{1,0:T(8,128)(2,1)S(1)}, bf16[256,4096]{1,0:T(8,128)(2,1)}, u32[]{:S(2)}) copy-start(bf16[256,4096]{1,0:T(8,128)(2,1)} %param.26) | copy-start | bytes 6291460
  (14 other events, 27.9 us)
Sparse Core Ops, SparseCore 0:
  41.6 51.7 all-gather.6
  95.9 46.6 all-gather.8
  144.5 45.5 all-gather.10
  306.0 54.0 reduce-scatter.3
  363.2 52.6 reduce-scatter.5
  419.3 52.6 reduce-scatter.7
  474.6 28.1 all-gather.12
  505.4 28.3 all-gather.14
  536.5 27.8 all-gather.16
where the time goes:
time: 581 us; the launch traced here: 575 us
  waiting for transfers between devices  157 us (27%)
  matrix products  147 us (25%)
  local copies, waits for them, and re-layouts  89.9 us (15%)
  other arithmetic  84.6 us (15%)
  starting transfers between devices  40.7 us (7%)
  blocking collectives  40.2 us (7%)
  between operations  15.8 us (3%)
    ppermute x9, waiting for transfers between devices, to_shard(): lax.ppermute(value, 'shard', [(i, (i + step) % group) for i in range(grou...  65.1 us
    dot_general x8, matrix products, matmul(): return jnp.dot(left, right, preferred_element_type=jnp.float32)  51.7 us
    ppermute x9, waiting for transfers between devices, from_shard(): lax.ppermute(value, 'shard', [(i, (i - step) % group) for i in range(grou...  46.6 us
    psum x1, blocking collectives, local(): small = lax.psum(small, ALL)  40.2 us
    unnamed x118, local copies, waits for them, and re-layouts  35 us
    dot_general x8, matrix products, outer_sum(): lax.dot_general(left, right, (((0,), (0,)), ((), ())), preferred_element_...  28.1 us
    reduce_scatter x1, waiting for transfers between devices, local(): lax.psum_scatter(grad_down.reshape(group, chips * part_down, model_width)...  27.2 us
    dot_general x8, matrix products, project_back(): lax.dot_general(left, right, (((1,), (1,)), ((), ())), preferred_element_...  25.8 us
  transfers between devices with their start and end apart: 35, of which 17 were waited for; matrix products, arithmetic and copies ran while one was open for 35% of the time, Pallas kernels for 0%

commit v1 on v0

--- a/solution.py
+++ b/solution.py
@@ -290,7 +290,7 @@
         grad_stwo,
     )
     small = jnp.concatenate([v.reshape(group, -1) for v in small], axis=1)
-    small = lax.psum(small, ALL)
+    small = jnp.sum(lax.all_gather(small, ALL), axis=0)
     small = lax.dynamic_index_in_dim(small, own, axis=0, keepdims=False)
     vecs, start = ([], 0)
     for size in sizes:

time: 581 us -> 644 us (1.11)
  waiting for transfers between devices: 157 us -> 258 us
  blocking collectives: 40.2 us -> 0 us
    all_gather x2, waiting for transfers between devices: 0.01 us -> 52.3 us  [scatter_columns(): return lax.all_gather(share, REP, axis=1, tiled=True).astype(jnp.float32)]
    psum x1 -> x0, blocking collectives: 40.2 us -> none  [local(): small = lax.psum(small, ALL)]
    all_gather x1, waiting for transfers between devices: 1.69 us -> 26.1 us  [local(): lax.all_gather(own_sum(grad_down), REP, axis=0, tiled=True)]
    all_gather x0 -> x1, waiting for transfers between devices: none -> 24.4 us  [local(): small = jnp.sum(lax.all_gather(small, ALL), axis=0)]
  transfers between devices with their start and end apart: 35 -> 36, of which waited for: 17 -> 20; matrix products, arithmetic and copies ran while one was open for 35% -> 32% of each run, Pallas kernels for 0% -> 0%
where the time goes in v1:
time: 644 us; the launch traced here: 638 us
  waiting for transfers between devices  258 us (40%)
  matrix products  147 us (23%)
  local copies, waits for them, and re-layouts  90.2 us (14%)
  other arithmetic  86.2 us (13%)
  starting transfers between devices  40.9 us (6%)
  between operations  16.2 us (3%)
    ppermute x9, waiting for transfers between devices, to_shard(): lax.ppermute(value, 'shard', [(i, (i + step) % group) for i in range(grou...  66.5 us
    all_gather x2, waiting for transfers between devices, scatter_columns(): return lax.all_gather(share, REP, axis=1, tiled=True).astype(jnp.float32)  52.3 us
    dot_general x8, matrix products, matmul(): return jnp.dot(left, right, preferred_element_type=jnp.float32)  51.8 us
    ppermute x9, waiting for transfers between devices, from_shard(): lax.ppermute(value, 'shard', [(i, (i - step) % group) for i in range(grou...  46.6 us
    unnamed x118, local copies, waits for them, and re-layouts  35.6 us
    dot_general x8, matrix products, outer_sum(): lax.dot_general(left, right, (((0,), (0,)), ((), ())), preferred_element_...  28.2 us
    reduce_scatter x1, waiting for transfers between devices, local(): lax.psum_scatter(grad_down.reshape(group, chips * part_down, model_width)...  27.2 us
    all_gather x1, waiting for transfers between devices, local(): lax.all_gather(own_sum(grad_down), REP, axis=0, tiled=True)  26.1 us
  transfers between devices with their start and end apart: 36, of which 20 were waited for; matrix products, arithmetic and copies ran while one was open for 32% of the time, Pallas kernels for 0%

profile of v1, /device:TPU:0, one launch (start us, length us, event | category | flops | bytes accessed | tf_op | source)
XLA Modules:
  0.0 638.5 jit_solution(5440367019682887224)
XLA Ops:
  15.2 3.1 collective-permute-start.2
  18.3 2.6 collective-permute-start.1
  22.3 5.7 collective-permute-done.2
  28.0 11.1 %collective-permute-done.1 = bf16[272,512]{1,0:T(8,128)(2,1)S(1)} collective-permute-done((bf16[272,512]{1,0:T(8,128)(2,1)S(1)}, bf16[272,512]{1,0:T(8,128)(2,1)S(1)}, u32[]{:S(2)}, u32[]{:S(2)}) %collective-permute-start.1) | collective-permute-done | bytes 278560 | tf_op jit(solution)/shard_map/ppermute | solution.py:130
  41.6 5.8 collective-permute-start.5
  49.8 6.6 %collective-permute-done.5 = bf16[256,512]{1,0:T(8,128)(2,1)S(1)} collective-permute-done((bf16[256,512]{1,0:T(8,128)(2,1)S(1)}, bf16[256,512]{1,0:T(8,128)(2,1)S(1)}, u32[]{:S(2)}, u32[]{:S(2)}) %collective-permute-start.5) | collective-permute-done | bytes 262176 | tf_op jit(solution)/shard_map/ppermute | solution.py:130
  56.4 9.4 %collective-permute-done.4 = bf16[256,512]{1,0:T(8,128)(2,1)S(1)} collective-permute-done((bf16[256,512]{1,0:T(8,128)(2,1)S(1)}, bf16[256,512]{1,0:T(8,128)(2,1)S(1)}, u32[]{:S(2)}, u32[]{:S(2)}) %collective-permute-start.4) | collective-permute-done | bytes 262176 | tf_op jit(solution)/shard_map/ppermute | solution.py:130
  68.6 6.1 collective-permute-start.8
  79.7 3.7 collective-permute-done.8
  83.4 10.0 %collective-permute-done.7 = bf16[128,1024]{1,0:T(8,128)(2,1)} collective-permute-done((bf16[128,1024]{1,0:T(8,128)(2,1)}, bf16[128,1024]{1,0:T(8,128)(2,1)}, u32[]{:S(2)}, u32[]{:S(2)}) %collective-permute-start.7) | collective-permute-done | bytes 262176 | tf_op jit(solution)/shard_map/ppermute | solution.py:130
  100.2 4.8 fusion.18
  114.8 9.4 %fusion.82 = (f32[16,512]{1,0:T(8,128)S(1)}, f32[16,512,512]{1,2,0:T(8,128)}) fusion(bf16[512,16,64]{0,2,1:T(8,128)(2,1)} %bitcast.175, bf16[512,16,64]{0,2,1:T(8,128)(2,1)S(1)} %bitcast.173, pred[512,512]{0,1:T(8,128)(4,1)S(1)} %compare_and_fusion), kind=kOutput, calls=%fused_computation.211 | convolution fusion | flops 549445632 | bytes 19169280 | tf_op jit(solution)/shard_map/qhd,khd->hqk/dot_general | solution.py:49
  124.3 8.4 %fusion = f32[16,512]{1,0:T(8,128)S(1)} fusion(f32[16,512,512]{1,2,0:T(8,128)} %get-tuple-element.65, f32[16,512]{1,0:T(8,128)S(1)} %get-tuple-element.64), kind=kLoop, calls=%fused_computation.10 | loop fusion | flops 8380416 | bytes 16842752 | tf_op jit(solution)/shard_map/reduce_sum | solution.py:55
  132.6 7.7 %fusion.42 = bf16[16,64,512]{2,1,0:T(8,128)(2,1)S(1)} fusion(bf16[512,16,64]{0,2,1:T(8,128)(2,1)S(1)} %bitcast.185, f32[16,512,512]{1,2,0:T(8,128)} %get-tuple-element.65, f32[16,512]{1,0:T(8,128)S(1)} %fusion, f32[16,512]{1,0:T(8,128)S(1)} %get-tuple-element.64), kind=kOutput, calls=%fused_computation.115 | convolution fusion | flops 549978112 | bytes 18939904 | tf_op jit(solution)/shard_map/hqk,khd->qhd/dot_general | solution.py:57
  140.3 2.8 fusion.55
  143.1 2.8 fusion.47
  149.9 4.6 fusion.67
  154.5 24.8 %multiply_convert_fusion.1 = (bf16[512,4096]{1,0:T(8,128)(2,1)S(1)}, f32[512,4096]{1,0:T(8,128)}) fusion(f32[4096]{0:T(1024)S(1)} %bitcast.220, f32[512,4096]{1,0:T(8,128)} %fusion.67, bf16[768,4096]{1,0:T(8,128)(2,1)} %all-gather.12.cloned.1.call-done, bf16[512,1024]{1,0:T(8,128)(2,1)S(1)} %fusion.54), kind=kOutput, calls=%fused_computation.25 | convolution fusion | flops 3361734656 | bytes 28065792 | tf_op jit(solution)/shard_map/dot_general | solution.py:21
  179.3 2.5 fusion.15
  183.8 2.6 fusion.57
  186.4 3.7 all-gather.14.cloned.1.call-done
  190.1 8.7 %fusion.84 = (f32[512]{0:T(512)S(1)}, f32[512,1024]{1,0:T(8,128)S(1)}) fusion(f32[1024]{0:T(1024)S(1)} %bitcast.222, f32[512,1024]{1,0:T(8,128)} %fusion.57, bf16[3072,1024]{1,0:T(8,128)(2,1)} %bitcast.231, bf16[512,4096]{1,0:T(8,128)(2,1)} %copy-done.6, f32[1024]{0:T(1024)S(1)} %bitcast.216, f32[1024]{0:T(1024)S(1)} %bitcast.209, f32[512]{0:T(512)S(1)} %fusion.72, ...), kind=kOutput, calls=%fused_computation.213 | convolution fusion | flops 3225419264 | bytes 15747072 | tf_op jit(solution)/shard_map/dot_general | solution.py:21
  202.2 6.1 fusion.86
  209.7 23.1 %convert_reduce_fusion = (f32[4096]{0:T(1024)S(1)}, bf16[512,4096]{1,0:T(8,128)(2,1)S(1)}) fusion(f32[512,4096]{1,0:T(8,128)S(1)} %bitcast.180, s32[]{:T(128)S(6)} %select_n.73, f32[512,3072]{1,0:T(8,128)S(1)} %fusion.86, f32[512,1024]{1,0:T(8,128)S(1)} %fusion.85), kind=kLoop, calls=%fused_computation.22 | loop fusion | flops 161476608 | bytes 20987908 | tf_op jit(solution)/shard_map/reduce_sum | solution.py:37
  234.3 5.9 fusion.88
  245.1 2.4 convolution_convert_fusion
  248.7 8.6 %convert_reduce_fusion.4 = (f32[16,64]{1,0:T(8,128)S(1)}, bf16[16,64,512]{2,1,0:T(8,128)(2,1)S(1)}) fusion(bf16[512,16,64]{0,2,1:T(8,128)(2,1)S(1)} %bitcast.177, f32[16,512,512]{1,2,0:T(8,128)} %get-tuple-element.65, f32[16,512]{1,0:T(8,128)S(1)} %log_add_fusion), kind=kOutput, calls=%fused_computation.100 | convolution fusion | flops 546831360 | bytes 18911232 | tf_op jit(solution)/shard_map/hqk,qhd->khd/dot_general | solution.py:85
  257.4 11.4 %multiply_reduce_fusion = (f32[16,512]{1,0:T(8,128)S(1)}, f32[16,512,512]{1,2,0:T(8,128)}) fusion(f32[16,512,512]{1,2,0:T(8,128)} %get-tuple-element.65, f32[16,512]{1,0:T(8,128)S(1)} %log_add_fusion, bf16[512,16,64]{0,2,1:T(8,128)(2,1)S(1)} %bitcast.178, bf16[512,16,64]{0,2,1:T(8,128)(2,1)S(1)} %bitcast.186), kind=kOutput, calls=%fused_computation.5 | convolution fusion | flops 549445632 | bytes 35717120 | tf_op jit(solution)/shard_map/qhd,khd->hqk/dot_general | solution.py:71
  268.8 12.0 %multiply_convert_fusion = bf16[16,512,512]{1,2,0:T(8,128)(2,1)S(1)} fusion(f32[16,512,512]{1,2,0:T(8,128)} %get-tuple-element.73, f32[16,512,512]{1,2,0:T(8,128)} %get-tuple-element.65, f32[16,512]{1,0:T(8,128)S(1)} %get-tuple-element.72, f32[16,512]{1,0:T(8,128)S(1)} %log_add_fusion), kind=kLoop, calls=%fused_computation.4 | loop fusion | flops 16777216 | bytes 42008576 | tf_op jit(solution)/shard_map/convert_element_type | solution.py:77
  280.8 2.6 multiply_convert_fusion.2
  294.5 3.1 fusion.89
  299.6 3.6 add_convert_fusion.3
  303.2 2.7 pad_maximum_fusion
  306.0 8.1 %reshape.403 = bf16[512,4,2,512]{3,2,1,0:T(2,128)(2,1)} reshape(bf16[512,4096]{1,0:T(8,128)(2,1)} %copy-done.7) | data formatting | bytes 8388608 | tf_op jit(solution)/shard_map/reshape | solution.py:209
  314.0 11.2 %constant_dynamic-slice_fusion.3 = (bf16[512,4,1,512]{3,2,1,0:T(2,128)(2,1)}, bf16[512,4,1,512]{3,2,1,0:T(2,128)(2,1)}) fusion(bf16[512,4,2,512]{3,2,1,0:T(2,128)(2,1)} %reshape.403, s32[]{:T(128)S(6)} %select_n.76, s32[]{:T(128)S(6)} %select_n.75), kind=kLoop, calls=%fused_computation.175 | loop fusion | bytes 8388616 | tf_op jit(solution)/shard_map/jit(dynamic_index_in_dim)/dynamic_slice | solution.py:210
  325.2 9.0 %copy.121 = bf16[512,4,1,512]{0,3,1,2:T(8,128)(2,1)S(1)} copy(bf16[512,4,1,512]{3,2,1,0:T(2,128)(2,1)} %get-tuple-element.34) | data formatting | bytes 4194304
  334.8 10.5 %copy.120 = bf16[512,4,1,512]{0,3,1,2:T(8,128)(2,1)} copy(bf16[512,4,1,512]{3,2,1,0:T(2,128)(2,1)} %get-tuple-element.35) | data formatting | bytes 4194304
  345.3 4.4 fusion.90
  349.8 6.3 add_convert_fusion.1
  356.1 6.5 %copy.109 = bf16[512,4096]{0,1:T(8,128)(2,1)} copy(bf16[512,4096]{1,0:T(8,128)(2,1)} %copy-done.6) | data formatting | bytes 8388608 | tf_op jit(solution)/shard_map/dynamic_slice | solution.py:140
  362.6 2.6 constant_dynamic-slice_fusion.1
  365.8 2.5 fusion.91
  368.3 2.7 collective-permute-done.22
  371.0 4.5 add_convert_fusion
  378.2 3.9 collective-permute-start.15
  383.0 5.9 collective-permute-done.15
  388.9 16.8 %collective-permute-done.14 = bf16[256,512]{1,0:T(8,128)(2,1)S(1)} collective-permute-done((bf16[256,512]{1,0:T(8,128)(2,1)S(1)}, bf16[256,512]{1,0:T(8,128)(2,1)S(1)}, u32[]{:S(2)}, u32[]{:S(2)}) %collective-permute-start.14) | collective-permute-done | bytes 262176 | tf_op jit(solution)/shard_map/ppermute | solution.py:133
  407.5 8.4 %reduce-scatter.6.cloned.1.call-done = bf16[1024,512]{1,0:T(8,128)(2,1)} async-done(((bf16[1024,2048]{1,0:T(8,128)(2,1)}), bf16[1024,512]{1,0:T(8,128)(2,1)}) %reduce-scatter.6.cloned.1.call-update) | async-done | bytes 1048592 | tf_op jit(solution)/shard_map/reduce_scatter | solution.py:230
  417.1 3.4 collective-permute-start.20
  421.6 5.7 collective-permute-done.20
  427.3 15.7 %collective-permute-done.19 = bf16[256,512]{1,0:T(8,128)(2,1)S(1)} collective-permute-done((bf16[256,512]{1,0:T(8,128)(2,1)S(1)}, bf16[256,512]{1,0:T(8,128)(2,1)S(1)}, u32[]{:S(2)}, u32[]{:S(2)}) %collective-permute-start.19) | collective-permute-done | bytes 262176 | tf_op jit(solution)/shard_map/ppermute | solution.py:133
  444.9 27.2 %reduce-scatter.8.cloned.1.call-done = bf16[4,128,1024]{2,1,0:T(8,128)(2,1)} async-done(((bf16[4,512,1024]{2,1,0:T(8,128)(2,1)}), bf16[4,128,1024]{2,1,0:T(8,128)(2,1)}) %reduce-scatter.8.cloned.1.call-update) | async-done | bytes 1048592 | tf_op jit(solution)/shard_map/reduce_scatter | solution.py:241
  473.3 3.4 collective-permute-start.25
  477.7 5.7 collective-permute-done.25
  483.4 16.8 %collective-permute-done.24 = bf16[128,1024]{1,0:T(8,128)(2,1)S(1)} collective-permute-done((bf16[128,1024]{1,0:T(8,128)(2,1)S(1)}, bf16[128,1024]{1,0:T(8,128)(2,1)S(1)}, u32[]{:S(2)}, u32[]{:S(2)}) %collective-permute-start.24) | collective-permute-done | bytes 262176 | tf_op jit(solution)/shard_map/ppermute | solution.py:133
  502.0 2.7 fusion.49
  504.8 5.2 fusion.16
  511.9 24.4 %all-gather.22.cloned.1.call-done = f32[32,4,3072]{2,1,0:T(4,128)} async-done(((f32[1,4,3072]{2,1,0:T(4,128)}), f32[32,4,3072]{2,1,0:T(4,128)}) %all-gather.22.cloned.1.call-update) | async-done | bytes 1572880 | tf_op jit(solution)/shard_map/all_gather | solution.py:293
  539.9 26.2 %all-gather.16.cloned.1.call-done = bf16[256,4096]{1,0:T(8,128)(2,1)} async-done(((bf16[256,512]{1,0:T(8,128)(2,1)}), bf16[256,4096]{1,0:T(8,128)(2,1)}) %all-gather.16.cloned.1.call-update) | async-done | bytes 2097168 | tf_op jit(solution)/shard_map/all_gather | solution.py:232
  566.1 3.6 slice.278
  570.7 26.2 %all-gather.18.cloned.1.call-done = bf16[256,4096]{1,0:T(8,128)(2,1)} async-done(((bf16[256,512]{1,0:T(8,128)(2,1)}), bf16[256,4096]{1,0:T(8,128)(2,1)}) %all-gather.18.cloned.1.call-update) | async-done | bytes 2097168 | tf_op jit(solution)/shard_map/all_gather | solution.py:232
  596.9 4.2 convert_element_type.279
  601.1 26.1 %all-gather.20.cloned.1.call-done = bf16[1024,1024]{1,0:T(8,128)(2,1)} async-done(((bf16[128,1024]{1,0:T(8,128)(2,1)}), bf16[1024,1024]{1,0:T(8,128)(2,1)}) %all-gather.20.cloned.1.call-update) | async-done | bytes 2097168 | tf_op jit(solution)/shard_map/all_gather | solution.py:247
  627.3 4.1 convert_element_type.287
  (257 shorter events, 90.3 us)
Async XLA Ops:
  7.2 34.3 %copy-start = (bf16[256,4096]{1,0:T(8,128)(2,1)S(1)}, bf16[256,4096]{1,0:T(8,128)(2,1)}, u32[]{:S(2)}) copy-start(bf16[256,4096]{1,0:T(8,128)(2,1)} %param.26) | copy-start | bytes 6291460
  7.2 93.0 %all-gather.10.cloned.1.call-start = ((), (), s32[]{:S(2)}) async-start(), calls=%async_computation.3 | async-start | bytes 7077888 | tf_op jit(solution)/shard_map/all_gather | solution.py:165
  15.2 62.5 %copy-start.17 = (bf16[1,512,1024]{2,1,0:T(8,128)(2,1)S(1)}, bf16[1,512,1024]{2,1,0:T(8,128)(2,1)}, u32[]{:S(2)}) copy-start(bf16[1,512,1024]{2,1,0:T(8,128)(2,1)} %param.16) | copy-start | bytes 3145732
  15.2 12.7 %collective-permute-start.2 = (bf16[272,512]{1,0:T(8,128)(2,1)S(1)}, bf16[272,512]{1,0:T(8,128)(2,1)S(1)}, u32[]{:S(2)}, u32[]{:S(2)}) collective-permute-start(bf16[272,512]{1,0:T(8,128)(2,1)S(1)} %pad_maximum_fusion.8), channel_id=1, source_target_pairs={{0,1},{1,2},{2,3},{3,0},{4,5},{5,6},{6,7},{7,4},{8,9},{9,10},{10,1... | collective-permute-start | bytes 835592 | tf_op jit(solution)/shard_map/ppermute | solution.py:130
  18.3 20.8 %collective-permute-start.1 = (bf16[272,512]{1,0:T(8,128)(2,1)S(1)}, bf16[272,512]{1,0:T(8,128)(2,1)S(1)}, u32[]{:S(2)}, u32[]{:S(2)}) collective-permute-start(bf16[272,512]{1,0:T(8,128)(2,1)S(1)} %pad_maximum_fusion.8), channel_id=1, source_target_pairs={{0,2},{1,3},{2,0},{3,1},{4,6},{5,7},{6,4},{7,5},{8,10},{9,11},{10,... | collective-permute-start | bytes 835592 | tf_op jit(solution)/shard_map/ppermute | solution.py:130
  20.9 18.2 %collective-permute-start = (bf16[272,512]{1,0:T(8,128)(2,1)S(1)}, bf16[272,512]{1,0:T(8,128)(2,1)S(1)}, u32[]{:S(2)}, u32[]{:S(2)}) collective-permute-start(bf16[272,512]{1,0:T(8,128)(2,1)S(1)} %pad_maximum_fusion.8), channel_id=1, source_target_pairs={{0,3},{1,0},{2,1},{3,2},{4,7},{5,4},{6,5},{7,6},{8,11},{9,8},{10,9... | collective-permute-start | bytes 835592 | tf_op jit(solution)/shard_map/ppermute | solution.py:130
  28.0 11.1 %copy-start.32 = (bf16[272,512]{1,0:T(8,128)(2,1)}, bf16[272,512]{1,0:T(8,128)(2,1)S(1)}, u32[]{:S(2)}) copy-start(bf16[272,512]{1,0:T(8,128)(2,1)S(1)} %collective-permute-done.2) | copy-start | bytes 835588
  39.1 40.3 %copy-start.40 = (s32[1,512]{1,0:T(1,128)S(1)}, s32[1,512]{1,0:T(1,128)}, u32[]{:S(2)}) copy-start(s32[1,512]{1,0:T(1,128)} %param.17) | copy-start | bytes 6148
  41.5 113.0 %all-gather.12.cloned.1.call-start = ((), (), s32[]{:S(2)}) async-start(), calls=%async_computation.4 | async-start | bytes 7077888 | tf_op jit(solution)/shard_map/all_gather | solution.py:168
  41.6 14.9 %collective-permute-start.5 = (bf16[256,512]{1,0:T(8,128)(2,1)S(1)}, bf16[256,512]{1,0:T(8,128)(2,1)S(1)}, u32[]{:S(2)}, u32[]{:S(2)}) collective-permute-start(bf16[256,512]{1,0:T(8,128)(2,1)S(1)} %constant_dynamic-slice_fusion.11), channel_id=1, source_target_pairs={{0,1},{1,2},{2,3},{3,0},{4,5},{5,6},{6,7},{7,4},{8,9},{9,10},{10,1... | collective-permute-start | bytes 786440 | tf_op jit(solution)/shard_map/ppermute | solution.py:130
  47.4 18.5 %collective-permute-start.4 = (bf16[256,512]{1,0:T(8,128)(2,1)S(1)}, bf16[256,512]{1,0:T(8,128)(2,1)S(1)}, u32[]{:S(2)}, u32[]{:S(2)}) collective-permute-start(bf16[256,512]{1,0:T(8,128)(2,1)S(1)} %constant_dynamic-slice_fusion.11), channel_id=1, source_target_pairs={{0,2},{1,3},{2,0},{3,1},{4,6},{5,7},{6,4},{7,5},{8,10},{9,11},{10,... | collective-permute-start | bytes 786440 | tf_op jit(solution)/shard_map/ppermute | solution.py:130
  49.6 16.2 %collective-permute-start.3 = (bf16[256,512]{1,0:T(8,128)(2,1)S(1)}, bf16[256,512]{1,0:T(8,128)(2,1)S(1)}, u32[]{:S(2)}, u32[]{:S(2)}) collective-permute-start(bf16[256,512]{1,0:T(8,128)(2,1)S(1)} %constant_dynamic-slice_fusion.11), channel_id=1, source_target_pairs={{0,3},{1,0},{2,1},{3,2},{4,7},{5,4},{6,5},{7,6},{8,11},{9,8},{10,9... | collective-permute-start | bytes 786440 | tf_op jit(solution)/shard_map/ppermute | solution.py:130
  66.8 123.2 %all-gather.14.cloned.1.call-start = ((), (), s32[]{:S(2)}) async-start(), calls=%async_computation.5 | async-start | bytes 7077888 | tf_op jit(solution)/shard_map/all_gather | solution.py:169
  68.6 14.8 %collective-permute-start.8 = (bf16[128,1024]{1,0:T(8,128)(2,1)}, bf16[128,1024]{1,0:T(8,128)(2,1)}, u32[]{:S(2)}, u32[]{:S(2)}) collective-permute-start(bf16[128,1024]{1,0:T(8,128)(2,1)} %constant_dynamic-slice_fusion.10), channel_id=1, source_target_pairs={{0,1},{1,2},{2,3},{3,0},{4,5},{5,6},{6,7},{7,4},{8,9},{9,10},{10,1... | collective-permute-start | bytes 786440 | tf_op jit(solution)/shard_map/ppermute | solution.py:130
  74.7 18.7 %collective-permute-start.7 = (bf16[128,1024]{1,0:T(8,128)(2,1)}, bf16[128,1024]{1,0:T(8,128)(2,1)}, u32[]{:S(2)}, u32[]{:S(2)}) collective-permute-start(bf16[128,1024]{1,0:T(8,128)(2,1)} %constant_dynamic-slice_fusion.10), channel_id=1, source_target_pairs={{0,2},{1,3},{2,0},{3,1},{4,6},{5,7},{6,4},{7,5},{8,10},{9,11},{10,... | collective-permute-start | bytes 786440 | tf_op jit(solution)/shard_map/ppermute | solution.py:130
  76.3 17.1 %collective-permute-start.6 = (bf16[128,1024]{1,0:T(8,128)(2,1)}, bf16[128,1024]{1,0:T(8,128)(2,1)}, u32[]{:S(2)}, u32[]{:S(2)}) collective-permute-start(bf16[128,1024]{1,0:T(8,128)(2,1)} %constant_dynamic-slice_fusion.10), channel_id=1, source_target_pairs={{0,3},{1,0},{2,1},{3,2},{4,7},{5,4},{6,5},{7,6},{8,11},{9,8},{10,9... | collective-permute-start | bytes 786440 | tf_op jit(solution)/shard_map/ppermute | solution.py:130
  95.5 281.5 %reduce-scatter.4.cloned.1.call-start = ((), (), s32[]{:S(2)}) async-start(), calls=%async_computation.6 | async-start | bytes 5242880 | tf_op jit(solution)/shard_map/reduce_scatter | solution.py:230
  100.2 4.8 copy-start.15
  114.8 9.4 %copy-start.8 = (bf16[512,1024]{0,1:T(8,128)(2,1)}, bf16[512,1024]{0,1:T(8,128)(2,1)S(1)}, u32[]{:S(2)}) copy-start(bf16[512,1024]{0,1:T(8,128)(2,1)S(1)} %copy.91) | copy-start | bytes 3145732
  124.3 8.4 %copy-start.19 = (bf16[512,1024]{0,1:T(8,128)(2,1)S(1)}, bf16[512,1024]{0,1:T(8,128)(2,1)}, u32[]{:S(2)}) copy-start(bf16[512,1024]{0,1:T(8,128)(2,1)} %copy.89) | copy-start | bytes 3145732
  149.9 4.6 copy-start.28
  179.3 4.5 copy-start.37
  190.0 9.1 %copy-start.11 = (bf16[1,512,1024]{2,1,0:T(8,128)(2,1)S(1)}, bf16[1,512,1024]{2,1,0:T(8,128)(2,1)}, u32[]{:S(2)}) copy-start(bf16[1,512,1024]{2,1,0:T(8,128)(2,1)} %param.19) | copy-start | bytes 3145732
  190.1 9.1 %copy-start.36 = (f32[1,2,4,128]{3,1,2,0:T(2,128)S(1)}, f32[1,2,4,128]{3,1,2,0:T(2,128)}, u32[]{:S(2)}) copy-start(f32[1,2,4,128]{3,1,2,0:T(2,128)} %copy.132) | copy-start | bytes 12292
  202.2 6.2 copy-start.30
  202.2 7.5 %slice-start = ((s8[8388608]{0:T(1024)(128)(4,1)}), s8[4194304]{0:T(1024)(128)(4,1)S(1)}, s32[]{:S(2)}) async-start(s8[8388608]{0:T(1024)(128)(4,1)} %bitcast.179), calls=%async_computation.13 | async-start | bytes 8388608
  202.2 6.2 copy-start.38
  202.2 7.5 %slice-start.1 = ((s8[8388608]{0:T(1024)(128)(4,1)}), s8[4194304]{0:T(1024)(128)(4,1)S(1)}, s32[]{:S(2)}) async-start(s8[8388608]{0:T(1024)(128)(4,1)} %bitcast.179), calls=%async_computation.14 | async-start | bytes 8388608
  232.8 7.4 %copy-start.7 = (bf16[512,4096]{1,0:T(8,128)(2,1)}, bf16[512,4096]{1,0:T(8,128)(2,1)S(1)}, u32[]{:S(2)}) copy-start(bf16[512,4096]{1,0:T(8,128)(2,1)S(1)} %get-tuple-element.22) | copy-start | bytes 12582916
  234.3 5.9 copy-start.3
  244.4 3.1 copy-start.25
  248.7 8.6 %copy-start.20 = (bf16[512,1024]{0,1:T(8,128)(2,1)S(1)}, bf16[512,1024]{0,1:T(8,128)(2,1)}, u32[]{:S(2)}) copy-start(bf16[512,1024]{0,1:T(8,128)(2,1)} %copy.89) | copy-start | bytes 3145732
  257.4 27.5 %copy-start.21 = (bf16[16,64,512]{2,1,0:T(8,128)(2,1)}, bf16[16,64,512]{2,1,0:T(8,128)(2,1)S(1)}, u32[]{:S(2)}) copy-start(bf16[16,64,512]{2,1,0:T(8,128)(2,1)S(1)} %get-tuple-element.75) | copy-start | bytes 3145732
  268.8 12.0 %copy-start.10 = (bf16[512,1024]{0,1:T(8,128)(2,1)S(1)}, bf16[512,1024]{0,1:T(8,128)(2,1)}, u32[]{:S(2)}) copy-start(bf16[512,1024]{0,1:T(8,128)(2,1)} %copy.90) | copy-start | bytes 3145732
  287.3 12.2 %collective-permute-start.10 = (bf16[512,1536]{0,1:T(8,128)(2,1)}, bf16[512,1536]{0,1:T(8,128)(2,1)}, u32[]{:S(2)}, u32[]{:S(2)}) collective-permute-start(bf16[512,1536]{0,1:T(8,128)(2,1)} %bitcast.26), channel_id=1, source_target_pairs={{0,4},{4,0},{1,5},{5,1},{2,6},{6,2},{3,7},{7,3},{8,12},{12,8},{9,1... | collective-permute-start | bytes 4718600 | tf_op jit(solution)/shard_map/ppermute | solution.py:136
  287.6 10.0 %collective-permute-start.11 = (bf16[512,1024]{0,1:T(8,128)(2,1)}, bf16[512,1024]{0,1:T(8,128)(2,1)}, u32[]{:S(2)}, u32[]{:S(2)}) collective-permute-start(bf16[512,1024]{0,1:T(8,128)(2,1)} %fusion.55), channel_id=1, source_target_pairs={{0,4},{4,0},{1,5},{5,1},{2,6},{6,2},{3,7},{7,3},{8,12},{12,8},{9,1... | collective-permute-start | bytes 3145736 | tf_op jit(solution)/shard_map/ppermute | solution.py:136
  287.9 11.7 %collective-permute-start.9 = (bf16[512,1024]{1,0:T(8,128)(2,1)}, bf16[512,1024]{1,0:T(8,128)(2,1)}, u32[]{:S(2)}, u32[]{:S(2)}) collective-permute-start(bf16[512,1024]{1,0:T(8,128)(2,1)} %fusion.56), channel_id=1, source_target_pairs={{0,4},{4,0},{1,5},{5,1},{2,6},{6,2},{3,7},{7,3},{8,12},{12,8},{9,1... | collective-permute-start | bytes 3145736 | tf_op jit(solution)/shard_map/ppermute | solution.py:136
  290.0 4.6 copy-start.29
  292.3 5.4 collective-permute-start.12
  305.9 110.0 %reduce-scatter.6.cloned.1.call-start = ((), (), s32[]{:S(2)}) async-start(), calls=%async_computation.8 | async-start | bytes 5242880 | tf_op jit(solution)/shard_map/reduce_scatter | solution.py:230
  334.2 15.5 %collective-permute-start.17 = (bf16[512,2048]{0,1:T(8,128)(2,1)S(1)}, bf16[512,2048]{0,1:T(8,128)(2,1)}, u32[]{:S(2)}, u32[]{:S(2)}) collective-permute-start(bf16[512,2048]{0,1:T(8,128)(2,1)S(1)} %bitcast.194), channel_id=1, source_target_pairs={{0,4},{4,0},{1,5},{5,1},{2,6},{6,2},{3,7},{7,3},{8,12},{12,8},{9,1... | collective-permute-start | bytes 6291464 | tf_op jit(solution)/shard_map/ppermute | solution.py:136
  334.6 15.1 %collective-permute-start.16 = (bf16[512,1024]{1,0:T(8,128)(2,1)}, bf16[512,1024]{1,0:T(8,128)(2,1)}, u32[]{:S(2)}, u32[]{:S(2)}) collective-permute-start(bf16[512,1024]{1,0:T(8,128)(2,1)} %copy-done.28), channel_id=1, source_target_pairs={{0,4},{4,0},{1,5},{5,1},{2,6},{6,2},{3,7},{7,3},{8,12},{12,8},{9,1... | collective-permute-start | bytes 3145736 | tf_op jit(solution)/shard_map/ppermute | solution.py:136
  356.1 116.0 %reduce-scatter.8.cloned.1.call-start = ((), (), s32[]{:S(2)}) async-start(), calls=%async_computation.10 | async-start | bytes 5242880 | tf_op jit(solution)/shard_map/reduce_scatter | solution.py:241
  362.6 3.1 copy-start.31
  365.3 5.7 collective-permute-start.21
  365.7 5.3 collective-permute-start.22
  375.5 160.8 %all-gather.22.cloned.1.call-start = ((), (), s32[]{:S(2)}) async-start(), calls=%async_computation.12 | async-start | bytes 1622016 | tf_op jit(solution)/shard_map/all_gather | solution.py:293
  376.7 189.3 %all-gather.16.cloned.1.call-start = ((), (), s32[]{:S(2)}) async-start(), calls=%async_computation.7 | async-start | bytes 2359296 | tf_op jit(solution)/shard_map/all_gather | solution.py:232
  378.2 123.8 %copy-start.14 = (bf16[16,64,512]{2,1,0:T(8,128)(2,1)S(1)}, bf16[16,64,512]{2,1,0:T(8,128)(2,1)}, u32[]{:S(2)}) copy-start(bf16[16,64,512]{2,1,0:T(8,128)(2,1)} %copy-done.13) | copy-start | bytes 3145732
  378.2 123.8 %copy-start.16 = (bf16[256,3072]{1,0:T(8,128)(2,1)S(1)}, bf16[256,3072]{1,0:T(8,128)(2,1)}, u32[]{:S(2)}) copy-start(bf16[256,3072]{1,0:T(8,128)(2,1)} %param.20) | copy-start | bytes 4718596
  378.2 10.6 %collective-permute-start.15 = (bf16[256,512]{1,0:T(8,128)(2,1)S(1)}, bf16[256,512]{1,0:T(8,128)(2,1)S(1)}, u32[]{:S(2)}, u32[]{:S(2)}) collective-permute-start(bf16[256,512]{1,0:T(8,128)(2,1)S(1)} %get-tuple-element.46), channel_id=1, source_target_pairs={{0,3},{1,0},{2,1},{3,2},{4,7},{5,4},{6,5},{7,6},{8,11},{9,8},{10,9... | collective-permute-start | bytes 786440 | tf_op jit(solution)/shard_map/ppermute | solution.py:133
  382.1 23.6 %collective-permute-start.14 = (bf16[256,512]{1,0:T(8,128)(2,1)S(1)}, bf16[256,512]{1,0:T(8,128)(2,1)S(1)}, u32[]{:S(2)}, u32[]{:S(2)}) collective-permute-start(bf16[256,512]{1,0:T(8,128)(2,1)S(1)} %get-tuple-element.47), channel_id=1, source_target_pairs={{0,2},{1,3},{2,0},{3,1},{4,6},{5,7},{6,4},{7,5},{8,10},{9,11},{10,... | collective-permute-start | bytes 786440 | tf_op jit(solution)/shard_map/ppermute | solution.py:133
  382.4 23.2 %collective-permute-start.13 = (bf16[256,512]{1,0:T(8,128)(2,1)S(1)}, bf16[256,512]{1,0:T(8,128)(2,1)S(1)}, u32[]{:S(2)}, u32[]{:S(2)}) collective-permute-start(bf16[256,512]{1,0:T(8,128)(2,1)S(1)} %get-tuple-element.45), channel_id=1, source_target_pairs={{0,1},{1,2},{2,3},{3,0},{4,5},{5,6},{6,7},{7,4},{8,9},{9,10},{10,1... | collective-permute-start | bytes 786440 | tf_op jit(solution)/shard_map/ppermute | solution.py:133
  407.5 189.4 %all-gather.18.cloned.1.call-start = ((), (), s32[]{:S(2)}) async-start(), calls=%async_computation.9 | async-start | bytes 2359296 | tf_op jit(solution)/shard_map/all_gather | solution.py:232
  417.1 10.1 %collective-permute-start.20 = (bf16[256,512]{1,0:T(8,128)(2,1)S(1)}, bf16[256,512]{1,0:T(8,128)(2,1)S(1)}, u32[]{:S(2)}, u32[]{:S(2)}) collective-permute-start(bf16[256,512]{1,0:T(8,128)(2,1)S(1)} %get-tuple-element.43), channel_id=1, source_target_pairs={{0,3},{1,0},{2,1},{3,2},{4,7},{5,4},{6,5},{7,6},{8,11},{9,8},{10,9... | collective-permute-start | bytes 786440 | tf_op jit(solution)/shard_map/ppermute | solution.py:133
  420.5 22.5 %collective-permute-start.19 = (bf16[256,512]{1,0:T(8,128)(2,1)S(1)}, bf16[256,512]{1,0:T(8,128)(2,1)S(1)}, u32[]{:S(2)}, u32[]{:S(2)}) collective-permute-start(bf16[256,512]{1,0:T(8,128)(2,1)S(1)} %get-tuple-element.44), channel_id=1, source_target_pairs={{0,2},{1,3},{2,0},{3,1},{4,6},{5,7},{6,4},{7,5},{8,10},{9,11},{10,... | collective-permute-start | bytes 786440 | tf_op jit(solution)/shard_map/ppermute | solution.py:133
  420.5 22.5 %collective-permute-start.18 = (bf16[256,512]{1,0:T(8,128)(2,1)S(1)}, bf16[256,512]{1,0:T(8,128)(2,1)S(1)}, u32[]{:S(2)}, u32[]{:S(2)}) collective-permute-start(bf16[256,512]{1,0:T(8,128)(2,1)S(1)} %get-tuple-element.42), channel_id=1, source_target_pairs={{0,1},{1,2},{2,3},{3,0},{4,5},{5,6},{6,7},{7,4},{8,9},{9,10},{10,1... | collective-permute-start | bytes 786440 | tf_op jit(solution)/shard_map/ppermute | solution.py:133
  444.8 182.5 %all-gather.20.cloned.1.call-start = ((), (), s32[]{:S(2)}) async-start(), calls=%async_computation.11 | async-start | bytes 2359296 | tf_op jit(solution)/shard_map/all_gather | solution.py:247
  473.3 10.1 %collective-permute-start.25 = (bf16[128,1024]{1,0:T(8,128)(2,1)S(1)}, bf16[128,1024]{1,0:T(8,128)(2,1)S(1)}, u32[]{:S(2)}, u32[]{:S(2)}) collective-permute-start(bf16[128,1024]{1,0:T(8,128)(2,1)S(1)} %get-tuple-element.40), channel_id=1, source_target_pairs={{0,3},{1,0},{2,1},{3,2},{4,7},{5,4},{6,5},{7,6},{8,11},{9,8},{10,9... | collective-permute-start | bytes 786440 | tf_op jit(solution)/shard_map/ppermute | solution.py:133
  476.6 23.5 %collective-permute-start.24 = (bf16[128,1024]{1,0:T(8,128)(2,1)S(1)}, bf16[128,1024]{1,0:T(8,128)(2,1)S(1)}, u32[]{:S(2)}, u32[]{:S(2)}) collective-permute-start(bf16[128,1024]{1,0:T(8,128)(2,1)S(1)} %get-tuple-element.41), channel_id=1, source_target_pairs={{0,2},{1,3},{2,0},{3,1},{4,6},{5,7},{6,4},{7,5},{8,10},{9,11},{10,... | collective-permute-start | bytes 786440 | tf_op jit(solution)/shard_map/ppermute | solution.py:133
  476.6 23.5 %collective-permute-start.23 = (bf16[128,1024]{1,0:T(8,128)(2,1)S(1)}, bf16[128,1024]{1,0:T(8,128)(2,1)S(1)}, u32[]{:S(2)}, u32[]{:S(2)}) collective-permute-start(bf16[128,1024]{1,0:T(8,128)(2,1)S(1)} %get-tuple-element.39), channel_id=1, source_target_pairs={{0,1},{1,2},{2,3},{3,0},{4,5},{5,6},{6,7},{7,4},{8,9},{9,10},{10,1... | collective-permute-start | bytes 786440 | tf_op jit(solution)/shard_map/ppermute | solution.py:133
  504.8 5.2 copy-start.5
  566.0 3.6 copy-start.12
  596.9 34.5 %copy-start.1 = (bf16[256,4096]{1,0:T(8,128)(2,1)S(1)}, bf16[256,4096]{1,0:T(8,128)(2,1)}, u32[]{:S(2)}) copy-start(bf16[256,4096]{1,0:T(8,128)(2,1)} %param.26) | copy-start | bytes 6291460
  (15 other events, 27.9 us)
Sparse Core Ops, SparseCore 0:
  41.6 51.7 all-gather.9
  95.9 46.6 all-gather.11
  144.5 45.5 all-gather.13
  306.0 54.1 reduce-scatter.3
  363.3 52.6 reduce-scatter.5
  419.4 52.6 reduce-scatter.7
  476.0 60.3 all-gather.21
  538.9 27.0 all-gather.15
  568.7 28.1 all-gather.17
  599.4 27.8 all-gather.19
